TPU v7x, 256 devices: a whole 4x4x8 slice. The times are simulated.
256 devices in a mesh: ctx: 16 (over z_hi, y), head: 16 (over x, z_lo, core).
Axes of the slice: x: 4, y: 4, z: 8 (z_hi: 4, z_lo: 2; z = z_hi * 2 + z_lo), core: 2. Of those that a mesh axis runs over, the one named last changes fastest.
Arguments:
- queries: bfloat16 [4096, 16384], P('ctx', 'head'), may hold values from -10 to 10
- key_states: bfloat16 [4096, 1024], P('ctx'), may hold values from -10 to 10
- value_states: bfloat16 [4096, 1024], P('ctx'), may hold values from -6 to 6
- vertical_blocks: int32 [128, 4], P('head'), may hold values from 0 to 31, as said below
- slash_offsets: int32 [128, 4], P('head'), may hold values from 0 to 31, as said below
- positions: int32 [4096], P('ctx'), may hold values from 0 to 32767, as said below
- out_weight: bfloat16 [16384, 16384], P('head', 'ctx'), may hold values from -0.25 to 0.25
Outputs:
- projected: bfloat16 [4096, 16384], P('head', 'ctx')
Inputs may be any that keep to these rules, and one draw needn't show every extreme that they name: `vertical_blocks`: each head's 4 vertical blocks are distinct. `slash_offsets`: each head's 4 offsets are distinct and the first of them is 0. `positions`: positions rise by one inside each block of 128 tokens; block b starts at a multiple of 128 at or after b * 1024 and before (b + 1) * 1024.
All inputs are finite; a program needn't handle non-finite values.
Results may differ from a plain program's by a relative error of at most 0.025.
Values may be sent and summed in bfloat16 or wider, within the bound.
A program may use at most 64 MiB of HBM per device.

v0:
```python
import math

import jax
import jax.numpy as jnp
from jax import lax
from jax.sharding import PartitionSpec as P

HD = 128
GROUP = 16
BLK = 128


def rotate_heads(states, positions):
    half_width = states.shape[-1] // 2
    exponents = jnp.arange(half_width, dtype=jnp.float32) * (2.0 / states.shape[-1])
    inverse_freq = 500000.0 ** (-exponents)
    angles = positions.astype(jnp.float32)[:, None] * inverse_freq[None, :]
    cosine = jnp.cos(angles)[:, None, :]
    sine_part = jnp.sin(angles)[:, None, :]
    front_half = states[..., :half_width]
    back_half = states[..., half_width:]
    return jnp.concatenate(
        [front_half * cosine - back_half * sine_part, back_half * cosine + front_half * sine_part],
        axis=-1,
    )


def per_device(
    queries, key_states, value_states, vertical_blocks, slash_offsets, positions, out_weight
):
    local_tokens = queries.shape[0]
    local_heads = queries.shape[1] // HD
    head_index = lax.axis_index("head")
    ctx_index = lax.axis_index("ctx")
    shared_head = head_index * local_heads // GROUP
    own_keys = lax.dynamic_slice_in_dim(key_states, shared_head * HD, HD, 1)
    own_values = lax.dynamic_slice_in_dim(value_states, shared_head * HD, HD, 1)
    rotated_own = rotate_heads(own_keys.astype(jnp.float32)[:, None, :], positions)[:, 0, :].astype(
        jnp.bfloat16
    )
    all_keys, all_values = (
        lax.all_gather(rotated_own, "ctx", axis=0, tiled=True),
        lax.all_gather(own_values, "ctx", axis=0, tiled=True),
    )
    query_rot = rotate_heads(
        queries.astype(jnp.float32).reshape(local_tokens, local_heads, HD), positions
    ).astype(jnp.bfloat16)
    query_blocks = local_tokens // BLK
    key_count = all_keys.shape[0] // BLK
    block_ids = ctx_index * query_blocks + jnp.arange(query_blocks, dtype=jnp.int32)
    vert_slots = jnp.broadcast_to(
        vertical_blocks[:, None, :], (local_heads, query_blocks, vertical_blocks.shape[1])
    )
    vert_valid = vert_slots <= block_ids[None, :, None]
    slash_slots = block_ids[None, :, None] - slash_offsets[:, None, :]
    repeated = jnp.any(slash_slots[..., None] == vertical_blocks[:, None, None, :], axis=-1)
    slash_valid = (slash_slots >= 0) & jnp.logical_not(repeated)
    slot_blocks = jnp.concatenate([vert_slots, slash_slots], axis=-1)
    slot_valid = jnp.concatenate([vert_valid, slash_valid], axis=-1)
    safe_blocks = jnp.clip(slot_blocks, 0, key_count - 1)
    key_tiles = all_keys.reshape(key_count, BLK, HD)[safe_blocks]
    value_tiles = all_values.reshape(key_count, BLK, HD)[safe_blocks]
    query_tiles = query_rot.reshape(query_blocks, BLK, local_heads, HD).transpose(2, 0, 1, 3)
    scores = jnp.einsum(
        "hqrd,hqskd->hqrsk", query_tiles, key_tiles, preferred_element_type=jnp.float32
    ) / math.sqrt(HD)
    diagonal = (slot_blocks == block_ids[None, :, None])[:, :, None, :, None]
    causal_pairs = (jnp.arange(BLK)[None, :] <= jnp.arange(BLK)[:, None])[None, None, :, None, :]
    allowed = slot_valid[:, :, None, :, None] & (jnp.logical_not(diagonal) | causal_pairs)
    masked = jnp.where(allowed, scores, -1e30)
    row_max = jnp.max(masked, axis=(3, 4), keepdims=True)
    exponentials = jnp.exp(masked - row_max)
    weights = (exponentials / jnp.sum(exponentials, axis=(3, 4), keepdims=True)).astype(
        jnp.bfloat16
    )
    attended = jnp.einsum(
        "hqrsk,hqskd->hqrd", weights, value_tiles, preferred_element_type=jnp.float32
    ).astype(jnp.bfloat16)
    head_out = attended.transpose(1, 2, 0, 3).reshape(local_tokens, local_heads * HD)
    partial_terms = jnp.dot(
        lax.all_gather(head_out, "ctx", axis=0, tiled=True),
        out_weight,
        preferred_element_type=jnp.float32,
    )
    projected = lax.psum_scatter(
        partial_terms.astype(jnp.bfloat16), "head", scatter_dimension=0, tiled=True
    )
    return projected


def solution(mesh):
    placed = (
        P("ctx", "head"),
        P("ctx", None),
        P("ctx", None),
        P("head", None),
        P("head", None),
        P("ctx"),
        P("head", "ctx"),
    )
    return jax.shard_map(
        per_device, mesh=mesh, in_specs=placed, out_specs=P("head", "ctx"), check_vma=False
    )
```

profile of v0, /device:TPU:20, one launch (start us, length us, event | category | flops | bytes accessed | tf_op | source)
XLA Modules:
  0.0 368.6 jit_solution(2328928914875954693)
XLA Ops:
  6.5 0.0 copy-start
  6.5 0.0 all-gather.9.cloned.1.call-start
  6.6 1.0 constant_dynamic-slice_fusion.1
  7.6 0.1 copy.56
  7.7 0.7 convert_element_type.25
  8.4 0.3 fusion.14
  8.7 0.6 pad_maximum_fusion
  9.3 0.0 all-gather.9.cloned.1.call-update
  9.4 0.0 all-gather.5.cloned.1.call-start
  9.4 1.5 constant_dynamic-slice_fusion
  10.9 0.0 all-gather.5.cloned.1.call-update
  10.9 0.0 all-gather.7.cloned.1.call-start
  11.0 0.8 broadcast_subtract_fusion
  11.7 0.7 broadcast_in_dim.15
  12.4 0.1 copy.46
  12.5 0.1 reshape.189
  12.6 0.7 compare_reduce_fusion
  13.3 0.8 broadcast_compare_fusion
  14.1 0.1 copy.41
  14.2 0.7 broadcast_in_dim.12
  14.9 0.1 fusion.17
  15.0 0.1 copy.42
  15.0 1.1 convert_bitcast_fusion
  16.2 0.2 copy.57
  16.4 0.5 multiply_cosine_fusion
  17.0 0.3 fusion.21
  17.3 1.4 subtract_convert_fusion
  18.7 46.9 %all-gather.9.cloned.1.call-done = bf16[4096,1,128]{0,2,1:T(8,128)(2,1)} async-done(((bf16[256,1,128]{0,2,1:T(8,128)(2,1)}), bf16[4096,1,128]{0,2,1:T(8,128)(2,1)}) %all-gather.9.cloned.1.call-update) | async-done | bytes 1048592 | tf_op jit(solution)/shard_map/all_gather | solution.py:42
  65.6 1.6 copy.53
  67.2 3.0 gather_fusion
  70.3 48.9 %all-gather.5.cloned.1.call-done = bf16[4096,128]{1,0:T(8,128)(2,1)} async-done(((bf16[256,128]{1,0:T(8,128)(2,1)}), bf16[4096,128]{1,0:T(8,128)(2,1)}) %all-gather.5.cloned.1.call-update) | async-done | bytes 1048592 | tf_op jit(solution)/shard_map/all_gather | solution.py:43
  119.2 4.4 %gather_fusion.1 = bf16[128,128,128]{2,1,0:T(8,128)(2,1)} fusion(bf16[32,128,128]{2,1,0:T(8,128)(2,1)} %bitcast.44, s32[1024]{0:T(1024)S(1)} %pad_clamp_fusion), kind=kCustom, calls=%fused_computation.1 | custom fusion | bytes 8389120 | tf_op jit(solution)/shard_map/gather | solution.py:62
  123.5 0.0 copy-done.2
  123.5 0.0 copy-done.3
  123.5 3.9 %fusion.1 = (f32[8,2,128]{2,1,0:T(2,128)S(1)}, f32[8,2,128,8,128]{2,4,3,1,0:T(8,128)S(1)}) fusion(pred[128,128]{0,1:T(8,128)(4,1)S(1)} %iota_compare_fusion, pred[8,2,8]{2,1,0:T(4,128)(4,1)S(1)} %copy.42, pred[8,2,8]{2,1,0:T(4,128)(4,1)S(1)} %copy.41, bf16[8,2,8,128,128]{4,3,2,1,0:T(8,128)(2,1)} %bitcast.47, bf16[2,128,8,64]{3,1,0,2:T(8,128)(2,1)S(1)} %bitcast.51, ...), kind=kOutput, calls=%fused_computation.7 | convolution fusion | flops 548403200 | bytes 13132032 | tf_op jit(solution)/shard_map/hqrd,hqskd->hqrsk/dot_general | solution.py:64
  127.4 0.0 copy-start.1
  127.4 3.0 fusion
  130.5 0.0 copy-done.1
  130.5 3.9 %fusion.5 = bf16[2,128,8,128]{3,1,0,2:T(8,128)(2,1)S(1)} fusion(bf16[8,2,8,128,128]{4,3,2,1,0:T(8,128)(2,1)S(1)} %bitcast.46, f32[8,2,128,8,128]{2,4,3,1,0:T(8,128)S(1)} %get-tuple-element.18, f32[8,2,128]{2,1,0:T(2,128)S(1)} %fusion, f32[8,2,128]{2,1,0:T(2,128)S(1)} %get-tuple-element.17, pred[128,128]{0,1:T(8,128)(4,1)S(1)} %iota_compare_fusion, ...), kind=kOutput, calls=%fused_computation.11 | convolution fusion | flops 551813120 | bytes 13140224 | tf_op jit(solution)/shard_map/hqrsk,hqskd->hqrd/dot_general | solution.py:76
  134.4 0.3 copy.49
  134.7 0.9 copy.64
  135.6 0.0 all-gather.7.cloned.1.call-update
  135.6 0.2 reduce-scatter.2.cloned.1.call-start
  135.9 101.5 %all-gather.7.cloned.1.call-done = bf16[4096,1024]{1,0:T(8,128)(2,1)} async-done(((bf16[256,1024]{1,0:T(8,128)(2,1)}), bf16[4096,1024]{1,0:T(8,128)(2,1)}) %all-gather.7.cloned.1.call-update) | async-done | bytes 8388624 | tf_op jit(solution)/shard_map/all_gather | solution.py:81
  237.3 0.0 copy-done
  237.3 14.5 %convolution_convert_fusion = bf16[4096,1024]{1,0:T(8,128)(2,1)} fusion(bf16[4096,1024]{1,0:T(8,128)(2,1)} %all-gather.7.cloned.1.call-done, bf16[1024,1024]{1,0:T(8,128)(2,1)S(1)} %copy-done), kind=kOutput, calls=%fused_computation.5 | convolution fusion | flops 8594128896 | bytes 18874368 | tf_op jit(solution)/shard_map/dot_general | solution.py:80
  251.8 0.0 reduce-scatter.2.cloned.1.call-update
  251.9 110.2 %reduce-scatter.2.cloned.1.call-done = bf16[256,1024]{1,0:T(8,128)(2,1)} async-done(((bf16[4096,1024]{1,0:T(8,128)(2,1)}), bf16[256,1024]{1,0:T(8,128)(2,1)}) %reduce-scatter.2.cloned.1.call-update) | async-done | bytes 524304 | tf_op jit(solution)/shard_map/reduce_scatter | solution.py:85
  (9 shorter events, 0.1 us)
Async XLA Ops:
  6.5 230.8 %copy-start = (bf16[1024,1024]{1,0:T(8,128)(2,1)S(1)}, bf16[1024,1024]{1,0:T(8,128)(2,1)}, u32[]{:S(2)}) copy-start(bf16[1024,1024]{1,0:T(8,128)(2,1)} %param.13) | copy-start | bytes 6291460
  6.5 59.1 %all-gather.9.cloned.1.call-start = ((), (), s32[]{:S(2)}) async-start(), calls=%async_computation.4 | async-start | bytes 1114112 | tf_op jit(solution)/shard_map/all_gather | solution.py:42
  9.4 109.8 %all-gather.5.cloned.1.call-start = ((), (), s32[]{:S(2)}) async-start(), calls=%async_computation.1 | async-start | bytes 1114112 | tf_op jit(solution)/shard_map/all_gather | solution.py:43
  10.9 226.4 %all-gather.7.cloned.1.call-start = ((), (), s32[]{:S(2)}) async-start(), calls=%async_computation.2 | async-start | bytes 8912896 | tf_op jit(solution)/shard_map/all_gather | solution.py:81
  119.2 4.4 %copy-start.2 = (bf16[256,8,64]{2,0,1:T(8,128)(2,1)S(1)}, bf16[256,8,64]{2,0,1:T(8,128)(2,1)}, u32[]{:S(2)}) copy-start(bf16[256,8,64]{2,0,1:T(8,128)(2,1)} %get-tuple-element.5) | copy-start | bytes 786436
  119.2 4.4 %copy-start.3 = (bf16[256,8,64]{2,0,1:T(8,128)(2,1)S(1)}, bf16[256,8,64]{2,0,1:T(8,128)(2,1)}, u32[]{:S(2)}) copy-start(bf16[256,8,64]{2,0,1:T(8,128)(2,1)} %get-tuple-element.6) | copy-start | bytes 786436
  127.4 3.0 copy-start.1
  135.6 226.4 %reduce-scatter.2.cloned.1.call-start = ((), (), s32[]{:S(2)}) async-start(), calls=%async_computation.3 | async-start | bytes 8912896 | tf_op jit(solution)/shard_map/reduce_scatter | solution.py:85
Sparse Core Ops, SparseCore 0:
  9.8 55.7 all-gather.8
  68.0 51.0 all-gather.4
  135.8 101.5 all-gather.6
  252.0 110.0 reduce-scatter.1
where the time goes:
time: 371 us; the launch traced here: 369 us
  waiting for transfers between devices  307 us (83%)
  matrix products  22.3 us (6%)
  local copies, waits for them, and re-layouts  15.1 us (4%)
  between operations  13.3 us (4%)
  other arithmetic  10.1 us (3%)
    reduce_scatter x1, waiting for transfers between devices, per_device(): lax.psum_scatter(partial_terms.astype(jnp.bfloat16), 'head', scatter_dime...  110 us
    all_gather x1, waiting for transfers between devices, per_device(): lax.all_gather(head_out, 'ctx', axis=0, tiled=True)  101 us
    all_gather x1, waiting for transfers between devices, per_device(): lax.all_gather(own_values, 'ctx', axis=0, tiled=True)  48.9 us
    all_gather x1, waiting for transfers between devices, per_device(): lax.all_gather(rotated_own, 'ctx', axis=0, tiled=True)  46.9 us
    dot_general x1, matrix products, per_device(): jnp.dot(lax.all_gather(head_out, 'ctx', axis=0, tiled=True), out_weight,...  14.5 us
  transfers between devices with their start and end apart: 4, of which 4 were waited for; matrix products, arithmetic and copies ran while one was open for 4% of the time, Pallas kernels for 0%

commit v1 on v0

--- a/solution.py
+++ b/solution.py
@@ -3,11 +3,354 @@
 import jax
 import jax.numpy as jnp
 from jax import lax
+from jax.experimental import pallas as pl
+from jax.experimental.pallas import tpu as pltpu
 from jax.sharding import PartitionSpec as P
 
 HD = 128
 GROUP = 16
 BLK = 128
+MESH = pl.DeviceIdType.MESH
+
+
+def place():
+    ctx = lax.axis_index("ctx")
+    head = lax.axis_index("head")
+    return ctx // 4, ctx % 4, head // 4, (head // 2) % 2, head % 2
+
+
+def device(zh, y, x, zl, core):
+    return {"ctx": zh * 4 + y, "head": x * 4 + zl * 2 + core}
+
+
+def remote(src, dst, send, recv, where):
+    return pltpu.make_async_remote_copy(
+        src_ref=src, dst_ref=dst, send_sem=send, recv_sem=recv, device_id=where, device_id_type=MESH
+    )
+
+
+def project_kernel(
+    own_ref, w_ref, out_ref, acts, weights, sib_out, sib_in, held, tree_out, leaf_in, root_in,
+    last_out, last_in, w_sem, w_send, w_recv, act_recv, z_send, y_send, sib_send, sib_recv,
+    leaf_send, leaf_recv, root_send, root_recv, last_send, last_recv,
+):
+    zh, y, x, zl, core = place()
+    mate = 3 - y
+    pair = y + 1 - 2 * (y % 2)
+    z_up = device((zh + 1) % 4, y, x, zl, core)
+    z_down = device((zh + 3) % 4, y, x, zl, core)
+    y_mate = device(zh, mate, x, zl, core)
+    y_pair = device(zh, pair, x, zl, core)
+    x_up = device(zh, y, (x + 1) % 4, zl, core)
+    x_down = device(zh, y, (x + 3) % 4, zl, core)
+    sibling = device(zh, y, x, zl, 1 - core)
+    half = sib_out.shape[2]
+    rows = acts.shape[1] // 2
+    tiles = half // 256
+
+    token_row = zl * 2 + core
+    near = jnp.where((token_row == y) | (token_row == 3 - y), 1, 0)
+    source_row = jnp.where(near == 1, y, pair)
+
+    barrier = pltpu.get_barrier_semaphore()
+
+    def greet(where):
+        pl.semaphore_signal(barrier, inc=1, device_id=where, device_id_type=MESH)
+
+    for where in (z_up, z_down, y_mate, y_pair, x_up, x_down, sibling):
+        greet(where)
+    for zs in range(2):
+        for cs in range(2):
+            @pl.when((near == 0) | (zs != zl) | (cs != core))
+            def _():
+                greet(device(zh, source_row, x, zs, cs))
+    pl.semaphore_wait(barrier, 11 - near)
+
+    def act_copy(src_slot, dst_slot, part, send, where):
+        return remote(
+            acts.at[src_slot, pl.ds(part * rows, rows)], acts.at[dst_slot, pl.ds(part * rows, rows)],
+            send, act_recv.at[dst_slot, part], where,
+        )
+
+    def act_wait(slot, part):
+        act_copy(slot, slot, part, z_send.at[0, 0], sibling).wait_recv()
+
+    to_up = lambda part: act_copy(0, 3, part, z_send.at[0, part], z_up)
+    to_down = lambda part: act_copy(0, 2, part, z_send.at[1, part], z_down)
+    on_up = lambda: act_copy(3, 6, 0, z_send.at[2, 0], z_up)
+    on_down = lambda: act_copy(2, 6, 1, z_send.at[2, 1], z_down)
+    y_slot = {0: 1, 2: 4, 3: 5, 6: 7}
+    to_mate = lambda slot, part: act_copy(slot, y_slot[slot], part, y_send.at[slot, part], y_mate)
+
+    w_own = pltpu.make_async_copy(w_ref, weights.at[0], w_sem)
+    w_own.start()
+    w_pair = remote(w_ref, weights.at[1], w_send, w_recv, y_pair)
+    w_pair.start()
+    acts[0] = own_ref[...]
+    to_up(0).start()
+    to_down(1).start()
+    to_mate(0, 0).start()
+    to_up(1).start()
+    to_down(0).start()
+    to_mate(0, 1).start()
+
+    def split(step):
+        slot = jnp.where(step < 7, step, jnp.where(step < 14, step - 7, 7))
+        w = jnp.where(step < 7, 0, jnp.where(step < 14, 1, step - 14))
+        ahead = jnp.where(slot < 2, 0, jnp.where(slot < 6, 1 + 2 * (slot % 2), 2))
+        group = jnp.where(slot < 2, slot, jnp.where(slot < 6, (slot - 2) // 2, slot - 6))
+        away = (x + 8 - zh - ahead) % 4
+        return slot, w, group, away
+
+    def leaf_copies(step, which):
+        return (
+            remote(
+                tree_out.at[step, pl.ds(0, rows)], leaf_in.at[which, 1],
+                leaf_send.at[which, 0], leaf_recv.at[which, 1], x_up,
+            ),
+            remote(
+                tree_out.at[step, pl.ds(rows, rows)], leaf_in.at[which, 0],
+                leaf_send.at[which, 1], leaf_recv.at[which, 0], x_down,
+            ),
+        )
+
+    def root_copy(step, which, side):
+        where = device(zh, y, (x + 3 + 2 * side) % 4, zl, core)
+        return remote(
+            tree_out.at[step], root_in.at[which, side], root_send.at[which, side],
+            root_recv.at[which, side], where,
+        )
+
+    def last_copy(w, group, which):
+        row = jnp.where(group == 0, y, mate)
+        column = jnp.where(w == 0, y, pair)
+        here = (w == 0) & (row // 2 == zl) & (row % 2 == core)
+        copy = remote(
+            last_out.at[which], last_in.at[zl * 2 + core], last_send.at[which],
+            last_recv.at[zl * 2 + core], device(zh, column, x, row // 2, row % 2),
+        )
+        return here, copy
+
+    def sib_copy(step):
+        return remote(
+            sib_out.at[step], sib_in.at[step], sib_send.at[step], sib_recv.at[step], sibling
+        )
+
+    def columns(part, tile):
+        return pl.ds(pl.multiple_of(part * half + tile * 256, 256), 256)
+
+    def product(slot, w, part, tile):
+        return jnp.dot(
+            acts[slot], weights[w, :, columns(part, tile)], preferred_element_type=jnp.float32
+        )
+
+    def tick(step, carry):
+        @pl.when(step == 1)
+        def _():
+            act_wait(3, 0)
+            on_up().start()
+            to_mate(3, 0).start()
+            act_wait(2, 1)
+            on_down().start()
+            to_mate(2, 1).start()
+
+        @pl.when(step == 2)
+        def _():
+            act_wait(2, 0)
+            to_mate(2, 0).start()
+            act_wait(3, 1)
+            to_mate(3, 1).start()
+
+        @pl.when(step == 4)
+        def _():
+            for part in range(2):
+                act_wait(6, part)
+                to_mate(6, part).start()
+
+        @pl.when((step == 1) | (step == 4) | (step == 5) | (step == 14))
+        def _():
+            slot = jnp.where(step == 14, 7, step)
+            act_wait(slot, 0)
+            act_wait(slot, 1)
+
+        @pl.when(step == 0)
+        def _():
+            w_own.wait()
+
+        @pl.when(step == 7)
+        def _():
+            w_pair.wait_recv()
+
+        @pl.when(step < 16)
+        def _():
+            slot, w, _, _ = split(step)
+
+            def give(tile, c):
+                sib_out[step, :, pl.ds(pl.multiple_of(tile * 256, 256), 256)] = product(
+                    slot, w, 1 - core, tile
+                ).astype(jnp.bfloat16)
+                return c
+
+            lax.fori_loop(0, tiles, give, 0)
+            sib_copy(step).start()
+
+            def keep(tile, c):
+                held[step % 4, :, pl.ds(pl.multiple_of(tile * 256, 256), 256)] = product(
+                    slot, w, core, tile
+                )
+                return c
+
+            lax.fori_loop(0, tiles, keep, 0)
+
+        @pl.when((step >= 1) & (step < 17))
+        def _():
+            old = step - 1
+            _, w, group, away = split(old)
+            which = group * 2 + w
+
+            @pl.when(away % 2 == 1)
+            def _():
+                side = away // 2
+                first = pl.multiple_of((1 - side) * rows, rows)
+                remote(
+                    leaf_in.at[which, side], leaf_in.at[which, side], leaf_send.at[which, 0],
+                    leaf_recv.at[which, side], sibling,
+                ).wait_recv()
+                tree_out[old, pl.ds(first, rows)] = (
+                    held[old % 4, pl.ds(first, rows)] + leaf_in[which, side].astype(jnp.float32)
+                ).astype(jnp.bfloat16)
+                other = pl.multiple_of(side * rows, rows)
+                tree_out[old, pl.ds(other, rows)] = held[old % 4, pl.ds(other, rows)].astype(
+                    jnp.bfloat16
+                )
+                root_copy(old, which, side).start()
+
+        @pl.when(step >= 2)
+        def _():
+            old = step - 2
+            _, w, group, away = split(old)
+            which = group * 2 + w
+
+            @pl.when(away == 0)
+            def _():
+                for side in range(2):
+                    root_copy(old, which, side).wait_recv()
+                last_out[which] = (
+                    held[old % 4]
+                    + root_in[which, 0].astype(jnp.float32)
+                    + root_in[which, 1].astype(jnp.float32)
+                ).astype(jnp.bfloat16)
+                here, copy = last_copy(w, group, which)
+
+                @pl.when(here)
+                def _():
+                    last_in[zl * 2 + core] = last_out[which]
+
+                @pl.when(jnp.logical_not(here))
+                def _():
+                    copy.start()
+
+        @pl.when(step < 16)
+        def _():
+            _, w, group, away = split(step)
+            which = group * 2 + w
+            sib_copy(step).wait_recv()
+
+            @pl.when(away == 2)
+            def _():
+                tree_out[step] = (held[step % 4] + sib_in[step].astype(jnp.float32)).astype(
+                    jnp.bfloat16
+                )
+                for copy in leaf_copies(step, which):
+                    copy.start()
+
+            @pl.when(away != 2)
+            def _():
+                held[step % 4] = held[step % 4] + sib_in[step].astype(jnp.float32)
+
+        return carry
+
+    lax.fori_loop(0, 18, tick, 0)
+
+    for zs in range(2):
+        for cs in range(2):
+            @pl.when((near == 0) | (zs != zl) | (cs != core))
+            def _():
+                remote(
+                    last_in.at[zs * 2 + cs], last_in.at[zs * 2 + cs], last_send.at[0],
+                    last_recv.at[zs * 2 + cs], sibling,
+                ).wait_recv()
+    for cs in range(2):
+        out_ref[:, cs * half:(cs + 1) * half] = (
+            last_in[cs].astype(jnp.float32) + last_in[2 + cs].astype(jnp.float32)
+        ).astype(jnp.bfloat16)
+
+    w_pair.wait_send()
+    for part in range(2):
+        to_up(part).wait_send()
+        to_down(part).wait_send()
+        for slot in y_slot:
+            to_mate(slot, part).wait_send()
+    on_up().wait_send()
+    on_down().wait_send()
+
+    def drain(step, carry):
+        _, w, group, away = split(step)
+        which = group * 2 + w
+        sib_copy(step).wait_send()
+
+        @pl.when(away == 2)
+        def _():
+            for copy in leaf_copies(step, which):
+                copy.wait_send()
+
+        @pl.when(away % 2 == 1)
+        def _():
+            root_copy(step, which, away // 2).wait_send()
+
+        @pl.when(away == 0)
+        def _():
+            here, copy = last_copy(w, group, which)
+
+            @pl.when(jnp.logical_not(here))
+            def _():
+                copy.wait_send()
+
+        return carry
+
+    lax.fori_loop(0, 16, drain, 0)
+
+
+def project(head_out, out_weight):
+    tokens, depth = head_out.shape
+    width = out_weight.shape[1]
+    half = width // 2
+    bf16 = jnp.bfloat16
+    dma = pltpu.SemaphoreType.DMA
+    return pl.pallas_call(
+        project_kernel,
+        out_shape=jax.ShapeDtypeStruct((tokens, width), bf16),
+        in_specs=[pl.BlockSpec(memory_space=pltpu.VMEM), pl.BlockSpec(memory_space=pl.ANY)],
+        out_specs=pl.BlockSpec(memory_space=pltpu.VMEM),
+        scratch_shapes=[
+            pltpu.VMEM((8, tokens, depth), bf16),
+            pltpu.VMEM((2, depth, width), bf16),
+            pltpu.VMEM((16, tokens, half), bf16),
+            pltpu.VMEM((16, tokens, half), bf16),
+            pltpu.VMEM((4, tokens, half), jnp.float32),
+            pltpu.VMEM((16, tokens, half), bf16),
+            pltpu.VMEM((4, 2, tokens // 2, half), bf16),
+            pltpu.VMEM((4, 2, tokens, half), bf16),
+            pltpu.VMEM((4, tokens, half), bf16),
+            pltpu.VMEM((4, tokens, half), bf16),
+            dma, dma, dma,
+            dma((8, 2)), dma((3, 2)), dma((8, 2)), dma((16,)), dma((16,)),
+            dma((4, 2)), dma((4, 2)), dma((4, 2)), dma((4, 2)), dma((4,)), dma((4,)),
+        ],
+        compiler_params=pltpu.CompilerParams(
+            collective_id=0, has_side_effects=True, vmem_limit_bytes=56 * 1024 * 1024
+        ),
+    )(head_out, out_weight)
 
 
 def rotate_heads(states, positions):
@@ -77,15 +420,7 @@
         "hqrsk,hqskd->hqrd", weights, value_tiles, preferred_element_type=jnp.float32
     ).astype(jnp.bfloat16)
     head_out = attended.transpose(1, 2, 0, 3).reshape(local_tokens, local_heads * HD)
-    partial_terms = jnp.dot(
-        lax.all_gather(head_out, "ctx", axis=0, tiled=True),
-        out_weight,
-        preferred_element_type=jnp.float32,
-    )
-    projected = lax.psum_scatter(
-        partial_terms.astype(jnp.bfloat16), "head", scatter_dimension=0, tiled=True
-    )
-    return projected
+    return project(head_out, out_weight)
 
 
 def solution(mesh):

time: 371 us -> 290 us (0.78)
  waiting for transfers between devices: 307 us -> 96.8 us
  Pallas kernels: 0 us -> 146 us
  matrix products: 22.3 us -> 7.75 us
    pallas_call x0 -> x1, Pallas kernels: none -> 146 us  [project(): pl.pallas_call(project_kernel, out_shape=jax.ShapeDtypeStruct((tokens, wi...]
    reduce_scatter x1 -> x0, waiting for transfers between devices: 110 us -> none  [per_device(): lax.psum_scatter(partial_terms.astype(jnp.bfloat16), 'head', scatter_dime...]
    all_gather x1 -> x0, waiting for transfers between devices: 101 us -> none  [per_device(): lax.all_gather(head_out, 'ctx', axis=0, tiled=True)]
    dot_general x1 -> x0, matrix products: 14.5 us -> none  [per_device(): jnp.dot(lax.all_gather(head_out, 'ctx', axis=0, tiled=True), out_weight,...]
  transfers between devices with their start and end apart: 4 -> 2, of which waited for: 4 -> 2; matrix products, arithmetic and copies ran while one was open for 4% -> 4% of each run, Pallas kernels for 0% -> 0%
where the time goes in v1:
time: 290 us
  Pallas kernels  146 us (50%)
  waiting for transfers between devices  96.8 us (33%)
  local copies, waits for them, and re-layouts  16.9 us (6%)
  between operations  13.6 us (5%)
  other arithmetic  9.15 us (3%)
  matrix products  7.75 us (3%)
    pallas_call x1, Pallas kernels, project(): pl.pallas_call(project_kernel, out_shape=jax.ShapeDtypeStruct((tokens, wi...  146 us
    all_gather x1, waiting for transfers between devices, per_device(): lax.all_gather(own_values, 'ctx', axis=0, tiled=True)  48.9 us
    all_gather x1, waiting for transfers between devices, per_device(): lax.all_gather(rotated_own, 'ctx', axis=0, tiled=True)  47.9 us
  transfers between devices with their start and end apart: 2, of which 2 were waited for; matrix products, arithmetic and copies ran while one was open for 4% of the time, Pallas kernels for 0%

profile of v1, /device:TPU:20, one launch (start us, length us, event | category | flops | bytes accessed | tf_op | source)
XLA Modules:
  0.0 289.9 jit_solution(17364983890692169883)
XLA Ops:
  6.5 0.0 copy-start
  6.5 0.0 all-gather.6.cloned.1.call-start
  6.6 1.0 copy-done
  7.6 0.1 copy.48
  7.7 0.7 convert_element_type.22
  8.4 0.3 fusion.14
  8.7 0.6 pad_maximum_fusion
  9.4 0.0 all-gather.6.cloned.1.call-update
  9.4 0.0 all-gather.4.cloned.1.call-start
  9.4 1.5 constant_dynamic-slice_fusion
  10.9 0.0 all-gather.4.cloned.1.call-update
  11.0 0.8 broadcast_subtract_fusion
  11.7 0.7 broadcast_in_dim.15
  12.4 0.1 copy.38
  12.5 0.1 reshape.189
  12.6 0.7 compare_reduce_fusion
  13.3 0.8 broadcast_compare_fusion
  14.1 0.1 copy.33
  14.2 0.7 broadcast_in_dim.12
  14.9 0.1 fusion.17
  15.0 0.1 copy.34
  15.0 1.1 convert_bitcast_fusion
  16.2 0.2 copy.49
  16.4 0.5 multiply_cosine_fusion
  17.0 0.3 fusion.21
  17.3 0.4 subtract_convert_fusion
  17.7 47.9 %all-gather.6.cloned.1.call-done = bf16[4096,1,128]{0,2,1:T(8,128)(2,1)} async-done(((bf16[256,1,128]{0,2,1:T(8,128)(2,1)}), bf16[4096,1,128]{0,2,1:T(8,128)(2,1)}) %all-gather.6.cloned.1.call-update) | async-done | bytes 1048592 | tf_op jit(solution)/shard_map/all_gather | solution.py:385
  65.6 1.6 copy.45
  67.2 3.1 %gather_fusion = bf16[128,128,128]{2,1,0:T(8,128)(2,1)} fusion(bf16[32,128,128]{2,1,0:T(8,128)(2,1)S(1)} %bitcast.41, s32[1024]{0:T(1024)S(1)} %pad_clamp_fusion), kind=kCustom, calls=%fused_computation | custom fusion | bytes 8389120 | tf_op jit(solution)/shard_map/gather | solution.py:404
  70.3 48.9 %all-gather.4.cloned.1.call-done = bf16[4096,128]{1,0:T(8,128)(2,1)} async-done(((bf16[256,128]{1,0:T(8,128)(2,1)}), bf16[4096,128]{1,0:T(8,128)(2,1)}) %all-gather.4.cloned.1.call-update) | async-done | bytes 1048592 | tf_op jit(solution)/shard_map/all_gather | solution.py:386
  119.2 4.3 %gather_fusion.1 = bf16[128,128,128]{2,1,0:T(8,128)(2,1)} fusion(bf16[32,128,128]{2,1,0:T(8,128)(2,1)} %bitcast.42, s32[1024]{0:T(1024)S(1)} %pad_clamp_fusion), kind=kCustom, calls=%fused_computation.1 | custom fusion | bytes 8389120 | tf_op jit(solution)/shard_map/gather | solution.py:405
  123.4 3.9 %fusion.1 = (f32[8,2,128]{2,1,0:T(2,128)S(1)}, f32[8,2,128,8,128]{2,4,3,1,0:T(8,128)S(1)}) fusion(pred[128,128]{0,1:T(8,128)(4,1)S(1)} %iota_compare_fusion, pred[8,2,8]{2,1,0:T(4,128)(4,1)S(1)} %copy.34, pred[8,2,8]{2,1,0:T(4,128)(4,1)S(1)} %copy.33, bf16[8,2,8,128,128]{4,3,2,1,0:T(8,128)(2,1)} %bitcast.45, bf16[2,128,8,64]{3,1,0,2:T(8,128)(2,1)S(1)} %bitcast.49, ...), kind=kOutput, calls=%fused_computation.6 | convolution fusion | flops 548403200 | bytes 13132032 | tf_op jit(solution)/shard_map/hqrd,hqskd->hqrsk/dot_general | solution.py:407
  127.3 0.0 copy-start.1
  127.3 3.0 %fusion = f32[8,2,128]{2,1,0:T(2,128)S(1)} fusion(f32[8,2,128,8,128]{2,4,3,1,0:T(8,128)S(1)} %get-tuple-element.18, f32[8,2,128]{2,1,0:T(2,128)S(1)} %get-tuple-element.17, pred[128,128]{0,1:T(8,128)(4,1)S(1)} %iota_compare_fusion, pred[8,2,8]{2,1,0:T(4,128)(4,1)S(1)} %copy.34, pred[8,2,8]{2,1,0:T(4,128)(4,1)S(1)} %copy.33), kind=kLoop, calls=%fused_computation.5 | loop fusion | flops 12580864 | bytes 8421632 | tf_op jit(solution)/shard_map/reduce_sum | solution.py:416
  130.4 0.0 copy-done.1
  130.4 3.8 %fusion.5 = bf16[2,128,8,128]{3,1,0,2:T(8,128)(2,1)S(1)} fusion(bf16[8,2,8,128,128]{4,3,2,1,0:T(8,128)(2,1)S(1)} %bitcast.44, f32[8,2,128,8,128]{2,4,3,1,0:T(8,128)S(1)} %get-tuple-element.18, f32[8,2,128]{2,1,0:T(2,128)S(1)} %fusion, f32[8,2,128]{2,1,0:T(2,128)S(1)} %get-tuple-element.17, pred[128,128]{0,1:T(8,128)(4,1)S(1)} %iota_compare_fusion, ...), kind=kOutput, calls=%fused_computation.10 | convolution fusion | flops 551813120 | bytes 13140224 | tf_op jit(solution)/shard_map/hqrsk,hqskd->hqrd/dot_general | solution.py:419
  134.2 0.3 copy.41
  134.6 0.9 copy.56
  135.5 145.7 %shard_map.73 = bf16[256,1024]{1,0:T(8,128)(2,1)} custom-call(bf16[256,1024]{1,0:T(8,128)(2,1)} %bitcast.47, bf16[1024,1024]{1,0:T(8,128)(2,1)} %w_ref.1), custom_call_target="tpu_custom_call" | custom-call | tf_op jit(solution)/shard_map/pallas_call | solution.py:330
  281.2 1.9 copy.58
  (8 shorter events, 0.1 us)
Async XLA Ops:
  6.5 1.0 copy-start
  6.5 59.1 %all-gather.6.cloned.1.call-start = ((), (), s32[]{:S(2)}) async-start(), calls=%async_computation.1 | async-start | bytes 1114112 | tf_op jit(solution)/shard_map/all_gather | solution.py:385
  9.4 109.8 %all-gather.4.cloned.1.call-start = ((), (), s32[]{:S(2)}) async-start(), calls=%async_computation | async-start | bytes 1114112 | tf_op jit(solution)/shard_map/all_gather | solution.py:386
  127.3 3.1 %copy-start.1 = (bf16[128,128,128]{2,1,0:T(8,128)(2,1)S(1)}, bf16[128,128,128]{2,1,0:T(8,128)(2,1)}, u32[]{:S(2)}) copy-start(bf16[128,128,128]{2,1,0:T(8,128)(2,1)} %gather_fusion.1) | copy-start | bytes 12582916
Sparse Core Ops, SparseCore 0:
  9.8 55.7 all-gather.5
  68.0 51.0 all-gather.3

commit v2 on v0

v2 whole, which is shorter than its diff:
```python
import math

import jax
import jax.numpy as jnp
from jax import lax
from jax.experimental import pallas as pl
from jax.experimental.pallas import tpu as pltpu
from jax.sharding import PartitionSpec as P

HD = 128
BLK = 128
MESH = pl.DeviceIdType.MESH
BF16 = jnp.bfloat16
F32 = jnp.float32

ORDER = (0, -1, -1, 1, -1, -1, 2, 3, 8, 9, 4, 5, 6, 10, 11, 12, 13, 14, 7, 15)
HOP2, HOP3, HOP4 = 2, 4, 6


def place():
    ctx = lax.axis_index("ctx")
    head = lax.axis_index("head")
    return ctx // 4, ctx % 4, head // 4, (head // 2) % 2, head % 2


def device(zh, y, x, zl, core):
    return {"ctx": (zh % 4) * 4 + y % 4, "head": (x % 4) * 4 + zl * 2 + core}


def remote(src, dst, send, recv, where):
    return pltpu.make_async_remote_copy(
        src_ref=src, dst_ref=dst, send_sem=send, recv_sem=recv, device_id=where, device_id_type=MESH
    )


def turned(states, cosine, sine):
    states = states.astype(F32)
    return (states * cosine + pltpu.roll(states, HD // 2, 1) * sine).astype(BF16)


def kernel(
    vert_ref, slash_ref, q_ref, cos_ref, sin_ref, k_ref, v_ref, w_ref, out_ref,
    k_own, v_own, q_rot, kv, acts, weights, sib_out, sib_in, held, chain_out, chain_in,
    last_out, last_in,
    own_sem, w_sem, w_send, w_recv, kz_send, kz_recv, ky_send, ky_recv, ks_send, ks_recv,
    act_recv, z_send, y_send, sib_send, sib_recv, chain_send, chain_recv, last_send, last_recv,
):
    zh, y, x, zl, core = place()
    mate = 3 - y
    pair = y + 1 - 2 * (y % 2)
    z_up = device(zh + 1, y, x, zl, core)
    z_down = device(zh + 3, y, x, zl, core)
    y_up = device(zh, y + 1, x, zl, core)
    y_down = device(zh, y + 3, x, zl, core)
    y_mate = device(zh, mate, x, zl, core)
    y_pair = device(zh, pair, x, zl, core)
    x_up = device(zh, y, x + 1, zl, core)
    x_down = device(zh, y, x + 3, zl, core)
    sibling = device(zh, y, x, zl, 1 - core)
    half = sib_out.shape[2]
    rows = acts.shape[1] // 2
    tiles = half // 256
    heads = q_ref.shape[1] // HD

    kv_column = pl.multiple_of((x * 2 + zl) * HD, HD)
    own_rows = pl.ds(pl.multiple_of(core * BLK, BLK), BLK)
    k_copy = pltpu.make_async_copy(
        k_ref.at[own_rows, pl.ds(kv_column, HD)], k_own, own_sem.at[0]
    )
    v_copy = pltpu.make_async_copy(
        v_ref.at[own_rows, pl.ds(kv_column, HD)], v_own, own_sem.at[1]
    )
    w_own = pltpu.make_async_copy(w_ref, weights.at[0], w_sem)
    k_copy.start()
    v_copy.start()
    w_own.start()

    token_row = zl * 2 + core
    near = jnp.where((token_row == y) | (token_row == mate), 1, 0)
    source_row = jnp.where(near == 1, y, pair)

    barrier = pltpu.get_barrier_semaphore()

    def greet(where):
        pl.semaphore_signal(barrier, inc=1, device_id=where, device_id_type=MESH)

    for where in (z_up, z_down, y_up, y_down, x_up, x_down, sibling):
        greet(where)
    for zs in range(2):
        for cs in range(2):
            @pl.when((near == 0) | (zs != zl) | (cs != core))
            def _():
                greet(device(zh, source_row, x, zs, cs))

    def block(dz, dy, which=core):
        return (((zh + dz) % 4) * 4 + (y + dy) % 4) * 2 + which

    mine = block(0, 0)
    k_copy.wait()
    v_copy.wait()
    kv[mine, 0] = turned(k_own[...], cos_ref[own_rows, :], sin_ref[own_rows, :])
    kv[mine, 1] = v_own[...].astype(F32).T.astype(BF16)
    pl.semaphore_wait(barrier, 11 - near)

    def kz_copy(dz_there, index, where):
        return remote(kv.at[mine], kv.at[mine], kz_send.at[index], kz_recv.at[dz_there], where)

    def kz_on(dz, part, where):
        here = kv.at[block(dz, 0), part]
        return remote(here, here, kz_send.at[2 + part], kz_recv.at[2 + part], where)

    def ky_copy(dz, dy, index, there, where):
        here = kv.at[block(dz, dy)]
        return remote(here, here, ky_send.at[dz, index], ky_recv.at[dz, there], where)

    def ks_copy(dz, dy):
        here = kv.at[block(dz, dy)]
        return remote(here, here, ks_send.at[dz, dy], ks_recv.at[dz, dy], sibling)

    def kv_row(dz):
        return (ky_copy(dz, 0, 0, 3, y_up), ky_copy(dz, 0, 1, 1, y_down), ks_copy(dz, 0))

    def kv_far(dz):
        if dz < 2:
            return ky_copy(dz, 3, 2, 2, y_up)
        return ky_copy(dz, 1, 2, 2, y_down)

    kz_sends = (kz_copy(1, 0, z_up), kz_copy(0, 1, z_down), kz_on(3, 0, z_up), kz_on(1, 1, z_down))
    kz_sends[0].start()
    kz_sends[1].start()
    for copy in kv_row(0):
        copy.start()

    for h in range(heads):
        column = slice(h * HD, (h + 1) * HD)
        q_rot[:, column] = turned(q_ref[:, column], cos_ref[...], sin_ref[...])

    kz_sends[1].wait_recv()
    kz_sends[3].start()
    for copy in kv_row(1):
        copy.start()
    kz_sends[0].wait_recv()
    kz_sends[2].start()
    for copy in kv_row(3):
        copy.start()

    def kv_near(dz):
        for dy in (3, 1):
            ky_copy(dz, dy, 0, dy, sibling).wait_recv()
            if (dy == 3) == (dz < 2):
                kv_far(dz).start()
            ks_copy(dz, dy).start()

    kv_near(0)
    kz_sends[2].wait_recv()
    kz_sends[3].wait_recv()
    for copy in kv_row(2):
        copy.start()
    kv_near(1)
    kv_near(3)
    w_pair = remote(w_ref, weights.at[1], w_send, w_recv, y_pair)
    w_pair.start()
    kv_near(2)
    for dz in range(4):
        ky_copy(dz, 2, 0, 2, sibling).wait_recv()
        ks_copy(dz, 2).start()
    for dz in range(4):
        for dy in range(4):
            ks_copy(dz, dy).wait_recv()

    def act_copy(src_slot, dst_slot, part, send, where):
        return remote(
            acts.at[src_slot, pl.ds(part * rows, rows)], acts.at[dst_slot, pl.ds(part * rows, rows)],
            send, act_recv.at[dst_slot, part], where,
        )

    def act_wait(slot, part):
        act_copy(slot, slot, part, z_send.at[0, 0], sibling).wait_recv()

    to_up = lambda part: act_copy(0, 3, part, z_send.at[0, part], z_up)
    to_down = lambda part: act_copy(0, 2, part, z_send.at[1, part], z_down)
    on_up = lambda: act_copy(3, 6, 0, z_send.at[2, 0], z_up)
    on_down = lambda: act_copy(2, 6, 1, z_send.at[2, 1], z_down)
    y_slot = {0: 1, 2: 4, 3: 5, 6: 7}
    to_mate = lambda slot, part: act_copy(slot, y_slot[slot], part, y_send.at[slot, part], y_mate)

    scale = math.log2(math.e) / math.sqrt(HD)
    ctx = zh * 4 + y

    def attend(part):
        here = ctx * 2 + part

        def one_head(h, carry):
            column = pl.ds(pl.multiple_of(h * HD, HD), HD)
            query = q_rot[part * BLK:(part + 1) * BLK, column]
            vertical = [vert_ref[h, s] for s in range(4)]
            blocks = [here] + vertical
            bias = [None] + [jnp.where(b < here, 0.0, -1e30) for b in vertical]
            for s in range(1, 4):
                b = here - slash_ref[h, s]
                seen = (b == vertical[0]) | (b == vertical[1]) | (b == vertical[2]) | (b == vertical[3])
                blocks.append(jnp.maximum(b, 0))
                bias.append(jnp.where((b >= 0) & jnp.logical_not(seen), 0.0, -1e30))
            keys = jnp.concatenate([kv[b, 0] for b in blocks], axis=0)
            values = jnp.concatenate([kv[b, 1] for b in blocks], axis=1)
            scores = lax.dot_general(
                keys, query, (((1,), (1,)), ((), ())), preferred_element_type=F32
            ) * scale
            tiles_of = [scores[s * BLK:(s + 1) * BLK] for s in range(8)]
            key_row = lax.broadcasted_iota(jnp.int32, (BLK, BLK), 0)
            query_row = lax.broadcasted_iota(jnp.int32, (BLK, BLK), 1)
            tiles_of[0] = jnp.where(key_row <= query_row, tiles_of[0], -1e30)
            top = jnp.max(tiles_of[0], axis=0, keepdims=True)
            for s in range(1, 8):
                top = jnp.maximum(top, jnp.max(tiles_of[s], axis=0, keepdims=True) + bias[s])
            powers = [jnp.exp2(tiles_of[0] - top)]
            for s in range(1, 8):
                powers.append(jnp.exp2(tiles_of[s] - (top - bias[s])))
            total = sum(jnp.sum(p, axis=0, keepdims=True) for p in powers)
            mixed = jnp.dot(
                values, jnp.concatenate([p.astype(BF16) for p in powers], axis=0),
                preferred_element_type=F32,
            )
            acts[0, part * BLK:(part + 1) * BLK, column] = (mixed * (1.0 / total)).T.astype(BF16)
            return carry

        lax.fori_loop(0, heads, one_head, 0)

    for part in range(2):
        attend(part)
        to_up(part).start()
        to_down(part).start()
        to_mate(0, part).start()

    def split(step):
        slot = step % 8
        ahead = jnp.where(slot < 2, 0, jnp.where(slot < 6, 1 + 2 * (slot % 2), 2))
        group = jnp.where(slot < 2, slot, jnp.where(slot < 6, (slot - 2) // 2, slot - 6))
        return slot, step // 8, group, (x + 8 - zh - ahead) % 4

    def chain_copy(step, part):
        here = pl.ds(part * rows, rows)
        return remote(
            chain_out.at[step, here], chain_in.at[step, here], chain_send.at[step, part],
            chain_recv.at[step, part], x_down if part else x_up,
        )

    def last_copy(w, group):
        which = group * 2 + w
        row = jnp.where(group == 0, y, mate)
        column = jnp.where(w == 0, y, pair)
        here = (w == 0) & (row // 2 == zl) & (row % 2 == core)
        copy = remote(
            last_out.at[which], last_in.at[zl * 2 + core], last_send.at[which],
            last_recv.at[zl * 2 + core], device(zh, column, x, row // 2, row % 2),
        )
        return here, copy

    def sib_copy(step):
        return remote(
            sib_out.at[step], sib_in.at[step], sib_send.at[step], sib_recv.at[step], sibling
        )

    def product(slot, w, side, tile):
        column = pl.ds(pl.multiple_of(side * half + tile * 256, 256), 256)
        return jnp.dot(acts[slot], weights[w, :, column], preferred_element_type=F32)

    def pass_on(step, spot, part):
        here = slice(part * rows, (part + 1) * rows)
        chain_copy(step, part).wait_recv()
        chain_out[step, here] = (held[spot, here] + chain_in[step, here].astype(F32)).astype(BF16)
        chain_copy(step, part).start()

    def work_at(position):
        step = jnp.int32(-1)
        for spot, entry in enumerate(ORDER):
            if entry >= 0:
                step = jnp.where(position == spot, entry, step)
        return step

    def tick(position, carry):
        step = work_at(position)
        slot, w, group, away = split(jnp.maximum(step, 0))
        spot = position % 8

        @pl.when(step == 1)
        def _():
            act_wait(3, 0)
            on_up().start()
            to_mate(3, 0).start()
            act_wait(2, 0)
            to_mate(2, 0).start()

        @pl.when(step == 2)
        def _():
            act_wait(2, 1)
            on_down().start()
            to_mate(2, 1).start()
            act_wait(3, 1)
            to_mate(3, 1).start()

        @pl.when(step == 4)
        def _():
            for part in range(2):
                act_wait(6, part)
                to_mate(6, part).start()

        @pl.when((step == 1) | (step == 4) | (step == 5) | (step == 7))
        def _():
            act_wait(slot, 0)
            act_wait(slot, 1)

        @pl.when(step == 0)
        def _():
            w_own.wait()

        @pl.when(step == 8)
        def _():
            w_pair.wait_recv()

        @pl.when(step >= 0)
        def _():
            def give(tile, c):
                sib_out[step, :, pl.ds(pl.multiple_of(tile * 256, 256), 256)] = product(
                    slot, w, 1 - core, tile
                ).astype(BF16)
                return c

            lax.fori_loop(0, tiles, give, 0)
            sib_copy(step).start()

            def keep(tile, c):
                held[spot, :, pl.ds(pl.multiple_of(tile * 256, 256), 256)] = product(
                    slot, w, core, tile
                )
                return c

            lax.fori_loop(0, tiles, keep, 0)

        two = work_at(position - HOP2)
        away_two = split(jnp.maximum(two, 0))[3]

        @pl.when((two >= 0) & (away_two == 2))
        def _():
            for part in range(2):
                pass_on(two, (position + 8 - HOP2) % 8, part)

        three = work_at(position - HOP3)
        away_three = split(jnp.maximum(three, 0))[3]

        @pl.when((three >= 0) & (away_three == 3))
        def _():
            pass_on(three, (position + 8 - HOP3) % 8, 0)

        @pl.when((three >= 0) & (away_three == 1))
        def _():
            pass_on(three, (position + 8 - HOP3) % 8, 1)

        four = work_at(position - HOP4)
        _, w_four, group_four, away_four = split(jnp.maximum(four, 0))

        @pl.when((four >= 0) & (away_four == 0))
        def _():
            which = group_four * 2 + w_four
            for part in range(2):
                chain_copy(four, part).wait_recv()
            last_out[which] = (
                held[(position + 8 - HOP4) % 8] + chain_in[four].astype(F32)
            ).astype(BF16)
            here, copy = last_copy(w_four, group_four)

            @pl.when(here)
            def _():
                last_in[zl * 2 + core] = last_out[which]

            @pl.when(jnp.logical_not(here))
            def _():
                copy.start()

        @pl.when(step >= 0)
        def _():
            sib_copy(step).wait_recv()
            held[spot] = held[spot] + sib_in[step].astype(F32)

            @pl.when(away == 1)
            def _():
                chain_out[step, 0:rows] = held[spot, 0:rows].astype(BF16)
                chain_copy(step, 0).start()

            @pl.when(away == 3)
            def _():
                chain_out[step, rows:] = held[spot, rows:].astype(BF16)
                chain_copy(step, 1).start()

        return carry

    lax.fori_loop(0, len(ORDER) + HOP4, tick, 0)

    for zs in range(2):
        for cs in range(2):
            @pl.when((near == 0) | (zs != zl) | (cs != core))
            def _():
                remote(
                    last_in.at[zs * 2 + cs], last_in.at[zs * 2 + cs], last_send.at[0],
                    last_recv.at[zs * 2 + cs], sibling,
                ).wait_recv()
    for cs in range(2):
        out_ref[:, cs * half:(cs + 1) * half] = (
            last_in[cs].astype(F32) + last_in[2 + cs].astype(F32)
        ).astype(BF16)

    w_pair.wait_send()
    for copy in kz_sends:
        copy.wait_send()
    for dz in range(4):
        for copy in kv_row(dz)[:2] + (kv_far(dz),):
            copy.wait_send()
        for dy in range(4):
            ks_copy(dz, dy).wait_send()
    for part in range(2):
        to_up(part).wait_send()
        to_down(part).wait_send()
        for slot in y_slot:
            to_mate(slot, part).wait_send()
    on_up().wait_send()
    on_down().wait_send()

    def drain(step, carry):
        _, w, group, away = split(step)
        sib_copy(step).wait_send()

        @pl.when(away != 0)
        def _():
            for part in range(2):
                chain_copy(step, part).wait_send()

        @pl.when(away == 0)
        def _():
            here, copy = last_copy(w, group)

            @pl.when(jnp.logical_not(here))
            def _():
                copy.wait_send()

        return carry

    lax.fori_loop(0, 16, drain, 0)


def per_device(
    queries, key_states, value_states, vertical_blocks, slash_offsets, positions, out_weight
):
    tokens, depth = queries.shape
    width = out_weight.shape[1]
    half = width // 2
    exponents = jnp.arange(HD // 2, dtype=F32) * (2.0 / HD)
    inverse_freq = 500000.0 ** (-exponents)
    angles = positions.astype(F32)[:, None] * inverse_freq[None, :]
    cosine = jnp.cos(angles)
    sine = jnp.sin(angles)
    cosine = jnp.concatenate([cosine, cosine], axis=1)
    sine = jnp.concatenate([-sine, sine], axis=1)
    vmem = pl.BlockSpec(memory_space=pltpu.VMEM)
    smem = pl.BlockSpec(memory_space=pltpu.SMEM)
    anywhere = pl.BlockSpec(memory_space=pl.ANY)
    dma = pltpu.SemaphoreType.DMA
    return pl.pallas_call(
        kernel,
        out_shape=jax.ShapeDtypeStruct((tokens, width), BF16),
        in_specs=[smem, smem, vmem, vmem, vmem, anywhere, anywhere, anywhere],
        out_specs=vmem,
        scratch_shapes=[
            pltpu.VMEM((BLK, HD), BF16),
            pltpu.VMEM((BLK, HD), BF16),
            pltpu.VMEM((tokens, depth), BF16),
            pltpu.VMEM((32, 2, BLK, HD), BF16),
            pltpu.VMEM((8, tokens, depth), BF16),
            pltpu.VMEM((2, depth, width), BF16),
            pltpu.VMEM((16, tokens, half), BF16),
            pltpu.VMEM((16, tokens, half), BF16),
            pltpu.VMEM((8, tokens, half), F32),
            pltpu.VMEM((16, tokens, half), BF16),
            pltpu.VMEM((16, tokens, half), BF16),
            pltpu.VMEM((4, tokens, half), BF16),
            pltpu.VMEM((4, tokens, half), BF16),
            dma((2,)), dma, dma, dma,
            dma((4,)), dma((4,)), dma((4, 3)), dma((4, 4)), dma((4, 4)), dma((4, 4)),
            dma((8, 2)), dma((3, 2)), dma((8, 2)), dma((16,)), dma((16,)),
            dma((16, 2)), dma((16, 2)), dma((4,)), dma((4,)),
        ],
        compiler_params=pltpu.CompilerParams(
            collective_id=0, has_side_effects=True, vmem_limit_bytes=56 * 1024 * 1024
        ),
    )(
        vertical_blocks, slash_offsets, queries, cosine, sine, key_states, value_states, out_weight
    )


def solution(mesh):
    placed = (
        P("ctx", "head"),
        P("ctx", None),
        P("ctx", None),
        P("head", None),
        P("head", None),
        P("ctx"),
        P("head", "ctx"),
    )
    return jax.shard_map(
        per_device, mesh=mesh, in_specs=placed, out_specs=P("head", "ctx"), check_vma=False
    )
```

time: 371 us -> 193 us (0.52)
  waiting for transfers between devices: 307 us -> 0 us
  Pallas kernels: 0 us -> 186 us
  matrix products: 22.3 us -> 0 us
  between operations: 13.3 us -> 0.02 us
  local copies, waits for them, and re-layouts: 15.1 us -> 4.55 us
  other arithmetic: 10.1 us -> 2.06 us
    all_gather x3 -> x0, waiting for transfers between devices: 197 us -> none  [the longest x1 101 us: per_device(): lax.all_gather(head_out, 'ctx', axis=0, tiled=True)]
    pallas_call x0 -> x1, Pallas kernels: none -> 186 us  [per_device(): pl.pallas_call(kernel, out_shape=jax.ShapeDtypeStruct((tokens, width), BF...]
    reduce_scatter x1 -> x0, waiting for transfers between devices: 110 us -> none  [per_device(): lax.psum_scatter(partial_terms.astype(jnp.bfloat16), 'head', scatter_dime...]
    dot_general x3 -> x0, matrix products: 22.3 us -> none  [the longest x1 14.5 us: per_device(): jnp.dot(lax.all_gather(head_out, 'ctx', axis=0, tiled=True), out_weight,...]
    gather x2 -> x0, local copies, waits for them, and re-layouts: 7.4 us -> none  [the longest x1 4.36 us: per_device(): value_tiles = all_values.reshape(key_count, BLK, HD)[safe_blocks]]
  transfers between devices with their start and end apart: 4 -> 0, of which waited for: 4 -> 0; matrix products, arithmetic and copies ran while one was open for 4% -> 0% of each run, Pallas kernels for 0% -> 0%
where the time goes in v2:
time: 193 us
  Pallas kernels  186 us (96%)
  local copies, waits for them, and re-layouts  4.55 us (2%)
  other arithmetic  2.06 us (1%)
    pallas_call x1, Pallas kernels, per_device(): pl.pallas_call(kernel, out_shape=jax.ShapeDtypeStruct((tokens, width), BF...  186 us
    unnamed x3, local copies, waits for them, and re-layouts  4.55 us

profile of v2, /device:TPU:20, one launch (start us, length us, event | category | flops | bytes accessed | tf_op | source)
XLA Modules:
  0.0 193.0 jit_solution(12983372439297100682)
XLA Ops:
  0.0 0.7 convert_element_type.3
  0.7 1.3 copy.8.vert_ref
  2.0 1.4 copy.9.slash_ref
  3.4 0.5 fusion
  3.9 0.8 pad_maximum_fusion
  4.8 186.3 %shard_map.73 = bf16[256,1024]{1,0:T(8,128)(2,1)} custom-call(s32[8,4]{1,0:T(8,128)} %copy.8.vert_ref, s32[8,4]{1,0:T(8,128)} %copy.9.slash_ref, bf16[256,1024]{1,0:T(8,128)(2,1)} %q_ref.1, f32[256,128]{1,0:T(8,128)} %get-tuple-element.8.cos_ref, f32[256,128]{1,0:T(8,128)} %get-tuple-element.9.sin_ref, bf16[256,1024]{1,0:T(8,128)(2,1)} %k_ref.1, ...), custom_call_target="tpu_custom_call" | custom-call | tf_op jit(solution)/shard_map/pallas_call | solution.py:467
  191.1 1.9 copy.11
  (1 shorter events, 0.0 us)

commit v3 on v2

--- a/solution.py
+++ b/solution.py
@@ -2,6 +2,7 @@
 
 import jax
 import jax.numpy as jnp
+import numpy as np
 from jax import lax
 from jax.experimental import pallas as pl
 from jax.experimental.pallas import tpu as pltpu
@@ -14,7 +15,7 @@
 F32 = jnp.float32
 
 ORDER = (0, -1, -1, 1, -1, -1, 2, 3, 8, 9, 4, 5, 6, 10, 11, 12, 13, 14, 7, 15)
-HOP2, HOP3, HOP4 = 2, 4, 6
+HOP2, HOP3, HOP4 = 3, 6, 9
 
 
 def place():
@@ -35,15 +36,15 @@
 
 def turned(states, cosine, sine):
     states = states.astype(F32)
-    return (states * cosine + pltpu.roll(states, HD // 2, 1) * sine).astype(BF16)
+    return states * cosine + pltpu.roll(states, HD // 2, 1) * sine
 
 
 def kernel(
-    vert_ref, slash_ref, q_ref, cos_ref, sin_ref, k_ref, v_ref, w_ref, out_ref,
-    k_own, v_own, q_rot, kv, acts, weights, sib_out, sib_in, held, chain_out, chain_in,
-    last_out, last_in,
+    vert_in, slash_in, pos_in, freq_ref, q_in, k_ref, v_ref, w_ref, last_in,
+    vert_ref, slash_ref, pos_ref, q_ref, k_own, v_own, q_rot, kv, acts, weights, held, chain_out,
+    chain_in, last_out,
     own_sem, w_sem, w_send, w_recv, kz_send, kz_recv, ky_send, ky_recv, ks_send, ks_recv,
-    act_recv, z_send, y_send, sib_send, sib_recv, chain_send, chain_recv, last_send, last_recv,
+    act_recv, as_send, as_recv, z_send, y_send, chain_send, chain_recv, last_send, last_recv,
 ):
     zh, y, x, zl, core = place()
     mate = 3 - y
@@ -54,25 +55,44 @@
     y_down = device(zh, y + 3, x, zl, core)
     y_mate = device(zh, mate, x, zl, core)
     y_pair = device(zh, pair, x, zl, core)
+    y_pair_sibling = device(zh, pair, x, zl, 1 - core)
     x_up = device(zh, y, x + 1, zl, core)
     x_down = device(zh, y, x + 3, zl, core)
     sibling = device(zh, y, x, zl, 1 - core)
-    half = sib_out.shape[2]
+    half = weights.shape[2]
+    depth = q_ref.shape[1]
     rows = acts.shape[1] // 2
     tiles = half // 256
     heads = q_ref.shape[1] // HD
 
     kv_column = pl.multiple_of((x * 2 + zl) * HD, HD)
     own_rows = pl.ds(pl.multiple_of(core * BLK, BLK), BLK)
-    k_copy = pltpu.make_async_copy(
-        k_ref.at[own_rows, pl.ds(kv_column, HD)], k_own, own_sem.at[0]
-    )
-    v_copy = pltpu.make_async_copy(
-        v_ref.at[own_rows, pl.ds(kv_column, HD)], v_own, own_sem.at[1]
-    )
-    w_own = pltpu.make_async_copy(w_ref, weights.at[0], w_sem)
-    k_copy.start()
-    v_copy.start()
+    small = [
+        pltpu.make_async_copy(src, dst, own_sem.at[i])
+        for i, (src, dst) in enumerate((
+            (pos_in, pos_ref),
+            (k_ref.at[own_rows, pl.ds(kv_column, HD)], k_own),
+            (v_ref.at[own_rows, pl.ds(kv_column, HD)], v_own),
+            (q_in, q_ref),
+            (vert_in, vert_ref),
+            (slash_in, slash_ref),
+        ))
+    ]
+    for copy in small:
+        copy.start()
+
+    depth_here = pl.ds(pl.multiple_of(core * depth, depth), depth)
+
+    def w_part(which):
+        return w_ref.at[:, pl.ds(pl.multiple_of(which * half, half), half)]
+
+    w_own = pltpu.make_async_copy(w_part(core), weights.at[0, depth_here], w_sem)
+    w_others = [
+        remote(w_part(which), weights.at[slot, depth_here], w_send.at[i], w_recv.at[i], where)
+        for i, (which, slot, where) in enumerate((
+            (1 - core, 0, sibling), (core, 1, y_pair), (1 - core, 1, y_pair_sibling),
+        ))
+    ]
     w_own.start()
 
     token_row = zl * 2 + core
@@ -84,7 +104,7 @@
     def greet(where):
         pl.semaphore_signal(barrier, inc=1, device_id=where, device_id_type=MESH)
 
-    for where in (z_up, z_down, y_up, y_down, x_up, x_down, sibling):
+    for where in (z_up, z_down, y_up, y_down, x_up, x_down, sibling, y_pair_sibling):
         greet(where)
     for zs in range(2):
         for cs in range(2):
@@ -96,11 +116,27 @@
         return (((zh + dz) % 4) * 4 + (y + dy) % 4) * 2 + which
 
     mine = block(0, 0)
-    k_copy.wait()
-    v_copy.wait()
-    kv[mine, 0] = turned(k_own[...], cos_ref[own_rows, :], sin_ref[own_rows, :])
+    small[0].wait()
+    lane = lax.broadcasted_iota(jnp.int32, (BLK, HD), 1)
+    row = lax.broadcasted_iota(jnp.int32, (BLK, HD), 0)
+    first = lane < HD // 2
+    start = jnp.where(first, pos_ref[0], pos_ref[BLK])
+    angles = (start + row).astype(F32) * freq_ref[0:1, :]
+    cosine = jnp.cos(angles)
+    sine = jnp.sin(angles)
+    cosine_other = pltpu.roll(cosine, HD // 2, 1)
+    sine_other = pltpu.roll(sine, HD // 2, 1)
+    tables = (
+        (jnp.where(first, cosine, cosine_other), jnp.where(first, -sine, sine_other)),
+        (jnp.where(first, cosine_other, cosine), jnp.where(first, -sine_other, sine)),
+    )
+    small[1].wait()
+    small[2].wait()
+    kv[mine, 0] = turned(
+        k_own[...], *(jnp.where(core == 0, one, two) for one, two in zip(*tables))
+    ).astype(BF16)
     kv[mine, 1] = v_own[...].astype(F32).T.astype(BF16)
-    pl.semaphore_wait(barrier, 11 - near)
+    pl.semaphore_wait(barrier, 12 - near)
 
     def kz_copy(dz_there, index, where):
         return remote(kv.at[mine], kv.at[mine], kz_send.at[index], kz_recv.at[dz_there], where)
@@ -131,9 +167,15 @@
     for copy in kv_row(0):
         copy.start()
 
-    for h in range(heads):
-        column = slice(h * HD, (h + 1) * HD)
-        q_rot[:, column] = turned(q_ref[:, column], cos_ref[...], sin_ref[...])
+    scale = math.log2(math.e) / math.sqrt(HD)
+    small[3].wait()
+    for part in range(2):
+        cosine, sine = (table * scale for table in tables[part])
+        for h in range(heads):
+            states = q_ref[part * BLK:(part + 1) * BLK, h * HD:(h + 1) * HD]
+            q_rot[part, h] = turned(states, cosine, sine).T.astype(BF16)
+    small[4].wait()
+    small[5].wait()
 
     kz_sends[1].wait_recv()
     kz_sends[3].start()
@@ -158,9 +200,9 @@
         copy.start()
     kv_near(1)
     kv_near(3)
-    w_pair = remote(w_ref, weights.at[1], w_send, w_recv, y_pair)
-    w_pair.start()
     kv_near(2)
+    for copy in w_others:
+        copy.start()
     for dz in range(4):
         ky_copy(dz, 2, 0, 2, sibling).wait_recv()
         ks_copy(dz, 2).start()
@@ -168,14 +210,21 @@
         for dy in range(4):
             ks_copy(dz, dy).wait_recv()
 
+    def act_at(slot, part):
+        return acts.at[slot, pl.ds(part * rows, rows), depth_here]
+
     def act_copy(src_slot, dst_slot, part, send, where):
         return remote(
-            acts.at[src_slot, pl.ds(part * rows, rows)], acts.at[dst_slot, pl.ds(part * rows, rows)],
-            send, act_recv.at[dst_slot, part], where,
+            act_at(src_slot, part), act_at(dst_slot, part), send, act_recv.at[dst_slot, part], where
         )
+
+    def share_copy(slot, part):
+        here = act_at(slot, part)
+        return remote(here, here, as_send.at[slot, part], as_recv.at[slot, part], sibling)
 
     def act_wait(slot, part):
         act_copy(slot, slot, part, z_send.at[0, 0], sibling).wait_recv()
+        share_copy(slot, part).start()
 
     to_up = lambda part: act_copy(0, 3, part, z_send.at[0, part], z_up)
     to_down = lambda part: act_copy(0, 2, part, z_send.at[1, part], z_down)
@@ -184,28 +233,24 @@
     y_slot = {0: 1, 2: 4, 3: 5, 6: 7}
     to_mate = lambda slot, part: act_copy(slot, y_slot[slot], part, y_send.at[slot, part], y_mate)
 
-    scale = math.log2(math.e) / math.sqrt(HD)
     ctx = zh * 4 + y
 
     def attend(part):
         here = ctx * 2 + part
 
         def one_head(h, carry):
-            column = pl.ds(pl.multiple_of(h * HD, HD), HD)
-            query = q_rot[part * BLK:(part + 1) * BLK, column]
-            vertical = [vert_ref[h, s] for s in range(4)]
+            column = pl.ds(pl.multiple_of(core * depth + h * HD, HD), HD)
+            vertical = [vert_ref[s, h] for s in range(4)]
             blocks = [here] + vertical
             bias = [None] + [jnp.where(b < here, 0.0, -1e30) for b in vertical]
             for s in range(1, 4):
-                b = here - slash_ref[h, s]
+                b = here - slash_ref[s, h]
                 seen = (b == vertical[0]) | (b == vertical[1]) | (b == vertical[2]) | (b == vertical[3])
                 blocks.append(jnp.maximum(b, 0))
                 bias.append(jnp.where((b >= 0) & jnp.logical_not(seen), 0.0, -1e30))
             keys = jnp.concatenate([kv[b, 0] for b in blocks], axis=0)
             values = jnp.concatenate([kv[b, 1] for b in blocks], axis=1)
-            scores = lax.dot_general(
-                keys, query, (((1,), (1,)), ((), ())), preferred_element_type=F32
-            ) * scale
+            scores = jnp.dot(keys, q_rot[part, h], preferred_element_type=F32)
             tiles_of = [scores[s * BLK:(s + 1) * BLK] for s in range(8)]
             key_row = lax.broadcasted_iota(jnp.int32, (BLK, BLK), 0)
             query_row = lax.broadcasted_iota(jnp.int32, (BLK, BLK), 1)
@@ -231,6 +276,7 @@
         to_up(part).start()
         to_down(part).start()
         to_mate(0, part).start()
+        share_copy(0, part).start()
 
     def split(step):
         slot = step % 8
@@ -245,25 +291,18 @@
             chain_recv.at[step, part], x_down if part else x_up,
         )
 
+    last_columns = pl.ds(pl.multiple_of(core * half, half), half)
+
     def last_copy(w, group):
         which = group * 2 + w
         row = jnp.where(group == 0, y, mate)
         column = jnp.where(w == 0, y, pair)
         here = (w == 0) & (row // 2 == zl) & (row % 2 == core)
         copy = remote(
-            last_out.at[which], last_in.at[zl * 2 + core], last_send.at[which],
+            last_out.at[which], last_in.at[zl, :, last_columns], last_send.at[which],
             last_recv.at[zl * 2 + core], device(zh, column, x, row // 2, row % 2),
         )
         return here, copy
-
-    def sib_copy(step):
-        return remote(
-            sib_out.at[step], sib_in.at[step], sib_send.at[step], sib_recv.at[step], sibling
-        )
-
-    def product(slot, w, side, tile):
-        column = pl.ds(pl.multiple_of(side * half + tile * 256, 256), 256)
-        return jnp.dot(acts[slot], weights[w, :, column], preferred_element_type=F32)
 
     def pass_on(step, spot, part):
         here = slice(part * rows, (part + 1) * rows)
@@ -281,7 +320,7 @@
     def tick(position, carry):
         step = work_at(position)
         slot, w, group, away = split(jnp.maximum(step, 0))
-        spot = position % 8
+        spot = position % 16
 
         @pl.when(step == 1)
         def _():
@@ -310,32 +349,41 @@
             act_wait(slot, 0)
             act_wait(slot, 1)
 
+        @pl.when((step >= 0) & (step < 8))
+        def _():
+            for part in range(2):
+                share_copy(slot, part).wait_recv()
+
         @pl.when(step == 0)
         def _():
             w_own.wait()
+            w_others[0].wait_recv()
 
         @pl.when(step == 8)
         def _():
-            w_pair.wait_recv()
+            w_others[1].wait_recv()
+            w_others[2].wait_recv()
 
         @pl.when(step >= 0)
         def _():
-            def give(tile, c):
-                sib_out[step, :, pl.ds(pl.multiple_of(tile * 256, 256), 256)] = product(
-                    slot, w, 1 - core, tile
-                ).astype(BF16)
-                return c
-
-            lax.fori_loop(0, tiles, give, 0)
-            sib_copy(step).start()
-
-            def keep(tile, c):
-                held[spot, :, pl.ds(pl.multiple_of(tile * 256, 256), 256)] = product(
-                    slot, w, core, tile
+            def one_tile(tile, c):
+                column = pl.ds(pl.multiple_of(tile * 256, 256), 256)
+                held[spot, :, column] = jnp.dot(
+                    acts[slot], weights[w, :, column], preferred_element_type=F32
                 )
                 return c
 
-            lax.fori_loop(0, tiles, keep, 0)
+            lax.fori_loop(0, tiles, one_tile, 0)
+
+            @pl.when(away == 1)
+            def _():
+                chain_out[step, 0:rows] = held[spot, 0:rows].astype(BF16)
+                chain_copy(step, 0).start()
+
+            @pl.when(away == 3)
+            def _():
+                chain_out[step, rows:] = held[spot, rows:].astype(BF16)
+                chain_copy(step, 1).start()
 
         two = work_at(position - HOP2)
         away_two = split(jnp.maximum(two, 0))[3]
@@ -343,18 +391,18 @@
         @pl.when((two >= 0) & (away_two == 2))
         def _():
             for part in range(2):
-                pass_on(two, (position + 8 - HOP2) % 8, part)
+                pass_on(two, (position + 16 - HOP2) % 16, part)
 
         three = work_at(position - HOP3)
         away_three = split(jnp.maximum(three, 0))[3]
 
         @pl.when((three >= 0) & (away_three == 3))
         def _():
-            pass_on(three, (position + 8 - HOP3) % 8, 0)
+            pass_on(three, (position + 16 - HOP3) % 16, 0)
 
         @pl.when((three >= 0) & (away_three == 1))
         def _():
-            pass_on(three, (position + 8 - HOP3) % 8, 1)
+            pass_on(three, (position + 16 - HOP3) % 16, 1)
 
         four = work_at(position - HOP4)
         _, w_four, group_four, away_four = split(jnp.maximum(four, 0))
@@ -365,32 +413,17 @@
             for part in range(2):
                 chain_copy(four, part).wait_recv()
             last_out[which] = (
-                held[(position + 8 - HOP4) % 8] + chain_in[four].astype(F32)
+                held[(position + 16 - HOP4) % 16] + chain_in[four].astype(F32)
             ).astype(BF16)
             here, copy = last_copy(w_four, group_four)
 
             @pl.when(here)
             def _():
-                last_in[zl * 2 + core] = last_out[which]
+                last_in[zl, :, last_columns] = last_out[which]
 
             @pl.when(jnp.logical_not(here))
             def _():
                 copy.start()
-
-        @pl.when(step >= 0)
-        def _():
-            sib_copy(step).wait_recv()
-            held[spot] = held[spot] + sib_in[step].astype(F32)
-
-            @pl.when(away == 1)
-            def _():
-                chain_out[step, 0:rows] = held[spot, 0:rows].astype(BF16)
-                chain_copy(step, 0).start()
-
-            @pl.when(away == 3)
-            def _():
-                chain_out[step, rows:] = held[spot, rows:].astype(BF16)
-                chain_copy(step, 1).start()
 
         return carry
 
@@ -401,15 +434,12 @@
             @pl.when((near == 0) | (zs != zl) | (cs != core))
             def _():
                 remote(
-                    last_in.at[zs * 2 + cs], last_in.at[zs * 2 + cs], last_send.at[0],
+                    last_out.at[0], last_in.at[zs, :, cs * half:(cs + 1) * half], last_send.at[0],
                     last_recv.at[zs * 2 + cs], sibling,
                 ).wait_recv()
-    for cs in range(2):
-        out_ref[:, cs * half:(cs + 1) * half] = (
-            last_in[cs].astype(F32) + last_in[2 + cs].astype(F32)
-        ).astype(BF16)
-
-    w_pair.wait_send()
+
+    for copy in w_others:
+        copy.wait_send()
     for copy in kz_sends:
         copy.wait_send()
     for dz in range(4):
@@ -422,12 +452,13 @@
         to_down(part).wait_send()
         for slot in y_slot:
             to_mate(slot, part).wait_send()
+        for slot in range(8):
+            share_copy(slot, part).wait_send()
     on_up().wait_send()
     on_down().wait_send()
 
     def drain(step, carry):
         _, w, group, away = split(step)
-        sib_copy(step).wait_send()
 
         @pl.when(away != 0)
         def _():
@@ -453,47 +484,43 @@
     tokens, depth = queries.shape
     width = out_weight.shape[1]
     half = width // 2
-    exponents = jnp.arange(HD // 2, dtype=F32) * (2.0 / HD)
-    inverse_freq = 500000.0 ** (-exponents)
-    angles = positions.astype(F32)[:, None] * inverse_freq[None, :]
-    cosine = jnp.cos(angles)
-    sine = jnp.sin(angles)
-    cosine = jnp.concatenate([cosine, cosine], axis=1)
-    sine = jnp.concatenate([-sine, sine], axis=1)
-    vmem = pl.BlockSpec(memory_space=pltpu.VMEM)
-    smem = pl.BlockSpec(memory_space=pltpu.SMEM)
+    inverse_freq = 500000.0 ** (-np.arange(HD // 2) * (2.0 / HD))
+    freq = jnp.asarray(np.tile(inverse_freq, (8, 2)), F32)
     anywhere = pl.BlockSpec(memory_space=pl.ANY)
     dma = pltpu.SemaphoreType.DMA
-    return pl.pallas_call(
+    pieces = pl.pallas_call(
         kernel,
-        out_shape=jax.ShapeDtypeStruct((tokens, width), BF16),
-        in_specs=[smem, smem, vmem, vmem, vmem, anywhere, anywhere, anywhere],
-        out_specs=vmem,
+        out_shape=jax.ShapeDtypeStruct((2, tokens, width), BF16),
+        in_specs=[anywhere] * 3 + [pl.BlockSpec(memory_space=pltpu.VMEM)] + [anywhere] * 4,
+        out_specs=pl.BlockSpec(memory_space=pltpu.VMEM),
         scratch_shapes=[
+            pltpu.SMEM(vertical_blocks.shape[::-1], jnp.int32),
+            pltpu.SMEM(slash_offsets.shape[::-1], jnp.int32),
+            pltpu.SMEM(positions.shape, jnp.int32),
+            pltpu.VMEM((tokens, depth), BF16),
             pltpu.VMEM((BLK, HD), BF16),
             pltpu.VMEM((BLK, HD), BF16),
-            pltpu.VMEM((tokens, depth), BF16),
+            pltpu.VMEM((2, depth // HD, HD, BLK), BF16),
             pltpu.VMEM((32, 2, BLK, HD), BF16),
-            pltpu.VMEM((8, tokens, depth), BF16),
-            pltpu.VMEM((2, depth, width), BF16),
-            pltpu.VMEM((16, tokens, half), BF16),
-            pltpu.VMEM((16, tokens, half), BF16),
-            pltpu.VMEM((8, tokens, half), F32),
+            pltpu.VMEM((8, tokens, 2 * depth), BF16),
+            pltpu.VMEM((2, 2 * depth, half), BF16),
+            pltpu.VMEM((16, tokens, half), F32),
             pltpu.VMEM((16, tokens, half), BF16),
             pltpu.VMEM((16, tokens, half), BF16),
             pltpu.VMEM((4, tokens, half), BF16),
-            pltpu.VMEM((4, tokens, half), BF16),
-            dma((2,)), dma, dma, dma,
+            dma((6,)), dma, dma((3,)), dma((3,)),
             dma((4,)), dma((4,)), dma((4, 3)), dma((4, 4)), dma((4, 4)), dma((4, 4)),
-            dma((8, 2)), dma((3, 2)), dma((8, 2)), dma((16,)), dma((16,)),
+            dma((8, 2)), dma((8, 2)), dma((8, 2)), dma((3, 2)), dma((8, 2)),
             dma((16, 2)), dma((16, 2)), dma((4,)), dma((4,)),
         ],
         compiler_params=pltpu.CompilerParams(
             collective_id=0, has_side_effects=True, vmem_limit_bytes=56 * 1024 * 1024
         ),
     )(
-        vertical_blocks, slash_offsets, queries, cosine, sine, key_states, value_states, out_weight
-    )
+        vertical_blocks.T, slash_offsets.T, positions, freq, queries, key_states, value_states,
+        out_weight,
+    ).astype(F32)
+    return (pieces[0] + pieces[1]).astype(BF16)
 
 
 def solution(mesh):

time: 193 us -> 139 us (0.72)
  Pallas kernels: 186 us -> 136 us
  local copies, waits for them, and re-layouts: 4.55 us -> 0 us
    pallas_call x1, Pallas kernels: 186 us -> 136 us  [per_device(): pl.pallas_call(kernel, out_shape=jax.ShapeDtypeStruct((2, tokens, width),...]
    unnamed x3 -> x0, local copies, waits for them, and re-layouts: 4.55 us -> none
where the time goes in v3:
time: 139 us; the launch traced here: 138 us
  Pallas kernels  136 us (98%)
  other arithmetic  2.4 us (2%)
    pallas_call x1, Pallas kernels, per_device(): pl.pallas_call(kernel, out_shape=jax.ShapeDtypeStruct((2, tokens, width),...  136 us

profile of v3, /device:TPU:20, one launch (start us, length us, event | category | flops | bytes accessed | tf_op | source)
XLA Modules:
  0.0 138.5 jit_solution(16200244480125738923)
XLA Ops:
  0.0 136.1 %shard_map.82 = bf16[2,256,1024]{2,1,0:T(8,128)(2,1)} custom-call(s32[4,8]{1,0:T(4,128)} %bitcast.4, s32[4,8]{1,0:T(4,128)} %bitcast.5, s32[256]{0:T(256)} %pos_in.1, f32[8,128]{1,0:T(8,128)} %constant.2.clone.freq_ref, bf16[256,1024]{1,0:T(8,128)(2,1)} %q_in.1, bf16[256,1024]{1,0:T(8,128)(2,1)} %k_ref.1, bf16[256,1024]{1,0:T(8,128)(2,1)} %v_ref.1, ...), custom_call_target="tpu_custom_call" | custom-call | tf_op jit(solution)/shard_map/pallas_call | solution.py:491
  136.1 1.5 %convert_element_type.9 = f32[2,256,1024]{2,1,0:T(8,128)S(1)} convert(bf16[2,256,1024]{2,1,0:T(8,128)(2,1)} %shard_map.82) | non-fusion elementwise | flops 524288 | bytes 3145728 | tf_op jit(solution)/shard_map/convert_element_type | solution.py:522
  137.5 0.9 fusion.1

commit v4 on v3

--- a/solution.py
+++ b/solution.py
@@ -14,8 +14,10 @@
 BF16 = jnp.bfloat16
 F32 = jnp.float32
 
-ORDER = (0, -1, -1, 1, -1, -1, 2, 3, 8, 9, 4, 5, 6, 10, 11, 12, 13, 14, 7, 15)
-HOP2, HOP3, HOP4 = 3, 6, 9
+HOP2, HOP3, HOP4 = 4, 9, 14
+PRODUCTS = 32
+PAUSES = 6
+CHUNKS = 4
 
 
 def place():
@@ -40,7 +42,7 @@
 
 
 def kernel(
-    vert_in, slash_in, pos_in, freq_ref, q_in, k_ref, v_ref, w_ref, last_in,
+    vert_in, slash_in, pos_in, freq_ref, q_in, k_ref, v_ref, w_ref, low_in, high_in,
     vert_ref, slash_ref, pos_ref, q_ref, k_own, v_own, q_rot, kv, acts, weights, held, chain_out,
     chain_in, last_out,
     own_sem, w_sem, w_send, w_recv, kz_send, kz_recv, ky_send, ky_recv, ks_send, ks_recv,
@@ -62,7 +64,7 @@
     half = weights.shape[2]
     depth = q_ref.shape[1]
     rows = acts.shape[1] // 2
-    tiles = half // 256
+    chunk = acts.shape[1] // CHUNKS
     heads = q_ref.shape[1] // HD
 
     kv_column = pl.multiple_of((x * 2 + zl) * HD, HD)
@@ -83,16 +85,18 @@
 
     depth_here = pl.ds(pl.multiple_of(core * depth, depth), depth)
 
-    def w_part(which):
-        return w_ref.at[:, pl.ds(pl.multiple_of(which * half, half), half)]
+    def w_part(which, start=0, size=half):
+        return w_ref.at[:, pl.ds(pl.multiple_of(which * half + start, 256), size)]
 
     w_own = pltpu.make_async_copy(w_part(core), weights.at[0, depth_here], w_sem)
-    w_others = [
-        remote(w_part(which), weights.at[slot, depth_here], w_send.at[i], w_recv.at[i], where)
-        for i, (which, slot, where) in enumerate((
-            (1 - core, 0, sibling), (core, 1, y_pair), (1 - core, 1, y_pair_sibling),
-        ))
-    ]
+    w_others = [remote(w_part(1 - core), weights.at[0, depth_here], w_send.at[0], w_recv.at[0], sibling)]
+    for start in (0, 256):
+        for which, where in ((core, y_pair), (1 - core, y_pair_sibling)):
+            i = len(w_others)
+            w_others.append(remote(
+                w_part(which, start, 256), weights.at[1, depth_here, pl.ds(start, 256)],
+                w_send.at[i], w_recv.at[i], where,
+            ))
     w_own.start()
 
     token_row = zl * 2 + core
@@ -211,7 +215,7 @@
             ks_copy(dz, dy).wait_recv()
 
     def act_at(slot, part):
-        return acts.at[slot, pl.ds(part * rows, rows), depth_here]
+        return acts.at[slot, pl.ds(part * chunk, chunk), depth_here]
 
     def act_copy(src_slot, dst_slot, part, send, where):
         return remote(
@@ -228,8 +232,8 @@
 
     to_up = lambda part: act_copy(0, 3, part, z_send.at[0, part], z_up)
     to_down = lambda part: act_copy(0, 2, part, z_send.at[1, part], z_down)
-    on_up = lambda: act_copy(3, 6, 0, z_send.at[2, 0], z_up)
-    on_down = lambda: act_copy(2, 6, 1, z_send.at[2, 1], z_down)
+    on_up = lambda part: act_copy(3, 6, part, z_send.at[2, part], z_up)
+    on_down = lambda part: act_copy(2, 6, part, z_send.at[2, part], z_down)
     y_slot = {0: 1, 2: 4, 3: 5, 6: 7}
     to_mate = lambda slot, part: act_copy(slot, y_slot[slot], part, y_send.at[slot, part], y_mate)
 
@@ -269,20 +273,47 @@
             acts[0, part * BLK:(part + 1) * BLK, column] = (mixed * (1.0 / total)).T.astype(BF16)
             return carry
 
-        lax.fori_loop(0, heads, one_head, 0)
+        lax.fori_loop(0, heads, one_head, 0, unroll=4)
 
     for part in range(2):
         attend(part)
         to_up(part).start()
         to_down(part).start()
-        to_mate(0, part).start()
-        share_copy(0, part).start()
+        for q in (2 * part, 2 * part + 1):
+            to_mate(0, q).start()
+            share_copy(0, q).start()
+
+    def send_later(q):
+        to_up(q - 2).wait_send()
+        to_down(q - 2).wait_send()
+        to_up(q).start()
+        to_down(q).start()
+
+    def forward(q):
+        act_wait(3, q)
+        to_mate(3, q).start()
+        act_wait(2, q)
+        to_mate(2, q).start()
+
+    def forward_far(q):
+        act_wait(6, q)
+        to_mate(6, q).start()
 
     def split(step):
-        slot = step % 8
-        ahead = jnp.where(slot < 2, 0, jnp.where(slot < 6, 1 + 2 * (slot % 2), 2))
-        group = jnp.where(slot < 2, slot, jnp.where(slot < 6, (slot - 2) // 2, slot - 6))
-        return slot, step // 8, group, (x + 8 - zh - ahead) % 4
+        third = lax.shift_right_arithmetic((step - 6) * 11, 5)
+        slot = jnp.where(step < 4, lax.shift_right_arithmetic(step, 1), step - 4)
+        tile = jnp.where(step < 4, lax.bitwise_and(step, 1), 2)
+        slot = jnp.where(step >= 6, 2 + third, slot)
+        tile = jnp.where(step >= 6, step - 6 - 3 * third, tile)
+        slot = jnp.where(step >= 21, step - 21, slot)
+        tile = jnp.where(step >= 21, 3, tile)
+        slot = jnp.where(step >= 28, 7, slot)
+        tile = jnp.where(step >= 28, step - 28, tile)
+        ahead = jnp.where(slot < 2, 0, jnp.where(slot < 6, 1 + 2 * lax.bitwise_and(slot, 1), 2))
+        group = jnp.where(
+            slot < 2, slot, jnp.where(slot < 6, lax.shift_right_arithmetic(slot - 2, 1), slot - 6)
+        )
+        return slot, tile, group, lax.bitwise_and(x + 8 - zh - ahead, 3)
 
     def chain_copy(step, part):
         here = pl.ds(part * rows, rows)
@@ -291,18 +322,30 @@
             chain_recv.at[step, part], x_down if part else x_up,
         )
 
-    last_columns = pl.ds(pl.multiple_of(core * half, half), half)
-
-    def last_copy(w, group):
-        which = group * 2 + w
+    def last_place(tile, group):
         row = jnp.where(group == 0, y, mate)
-        column = jnp.where(w == 0, y, pair)
-        here = (w == 0) & (row // 2 == zl) & (row % 2 == core)
-        copy = remote(
-            last_out.at[which], last_in.at[zl, :, last_columns], last_send.at[which],
-            last_recv.at[zl * 2 + core], device(zh, column, x, row // 2, row % 2),
+        column = jnp.where(tile < 2, y, pair)
+        here = (tile < 2) & (row // 2 == zl) & (row % 2 == core)
+        columns = pl.ds(pl.multiple_of(core * half + (tile % 2) * 256, 256), 256)
+        return here, device(zh, column, x, row // 2, row % 2), group * 4 + tile, columns
+
+    def last_copy(tile, group, zs):
+        _, where, which, columns = last_place(tile, group)
+        return remote(
+            last_out.at[which], (low_in, high_in)[zs].at[:, columns], last_send.at[which],
+            last_recv.at[zs * 2 + core, tile % 2], where,
         )
-        return here, copy
+
+    def send_last(tile, group):
+        here, _, which, columns = last_place(tile, group)
+        for zs, target in enumerate((low_in, high_in)):
+            @pl.when(here & (zl == zs))
+            def _():
+                target[:, columns] = last_out[which]
+
+            @pl.when(jnp.logical_not(here) & (zl == zs))
+            def _():
+                last_copy(tile, group, zs).start()
 
     def pass_on(step, spot, part):
         here = slice(part * rows, (part + 1) * rows)
@@ -311,69 +354,73 @@
         chain_copy(step, part).start()
 
     def work_at(position):
-        step = jnp.int32(-1)
-        for spot, entry in enumerate(ORDER):
-            if entry >= 0:
-                step = jnp.where(position == spot, entry, step)
+        step = jnp.where(position < 2, position, -1)
+        step = jnp.where((position >= 5) & (position < 7), position - 3, step)
+        step = jnp.where((position >= 10) & (position < PRODUCTS + PAUSES), position - PAUSES, step)
         return step
 
     def tick(position, carry):
         step = work_at(position)
-        slot, w, group, away = split(jnp.maximum(step, 0))
-        spot = position % 16
-
-        @pl.when(step == 1)
-        def _():
-            act_wait(3, 0)
-            on_up().start()
-            to_mate(3, 0).start()
-            act_wait(2, 0)
-            to_mate(2, 0).start()
+        slot, tile, group, away = split(jnp.maximum(step, 0))
+        spot = lax.bitwise_and(position, 15)
 
         @pl.when(step == 2)
         def _():
-            act_wait(2, 1)
-            on_down().start()
-            to_mate(2, 1).start()
-            act_wait(3, 1)
-            to_mate(3, 1).start()
+            forward(1)
 
         @pl.when(step == 4)
         def _():
-            for part in range(2):
-                act_wait(6, part)
-                to_mate(6, part).start()
-
-        @pl.when((step == 1) | (step == 4) | (step == 5) | (step == 7))
-        def _():
-            act_wait(slot, 0)
-            act_wait(slot, 1)
-
-        @pl.when((step >= 0) & (step < 8))
-        def _():
-            for part in range(2):
-                share_copy(slot, part).wait_recv()
+            forward(2)
+            on_up(0).start()
+            on_down(2).start()
+
+        @pl.when(step == 6)
+        def _():
+            forward(3)
+            on_up(1).start()
+            on_down(3).start()
+
+        @pl.when(step == 10)
+        def _():
+            forward_far(0)
+            forward_far(2)
+
+        @pl.when(step == 12)
+        def _():
+            forward_far(1)
+            forward_far(3)
+
+        @pl.when((step == 2) | (step == 12) | (step == 15) | (step == 28))
+        def _():
+            for q in range(CHUNKS):
+                act_wait(slot, q)
+
+        @pl.when((step >= 0) & (tile == 0))
+        def _():
+            for q in range(CHUNKS):
+                share_copy(slot, q).wait_recv()
 
         @pl.when(step == 0)
         def _():
             w_own.wait()
             w_others[0].wait_recv()
 
-        @pl.when(step == 8)
+        @pl.when(step == 4)
         def _():
             w_others[1].wait_recv()
             w_others[2].wait_recv()
 
+        @pl.when(step == 21)
+        def _():
+            w_others[3].wait_recv()
+            w_others[4].wait_recv()
+
         @pl.when(step >= 0)
         def _():
-            def one_tile(tile, c):
-                column = pl.ds(pl.multiple_of(tile * 256, 256), 256)
-                held[spot, :, column] = jnp.dot(
-                    acts[slot], weights[w, :, column], preferred_element_type=F32
-                )
-                return c
-
-            lax.fori_loop(0, tiles, one_tile, 0)
+            column = pl.ds(pl.multiple_of(lax.bitwise_and(tile, 1) * 256, 256), 256)
+            held[spot] = jnp.dot(
+                acts[slot], weights[lax.shift_right_arithmetic(tile, 1), :, column], preferred_element_type=F32
+            )
 
             @pl.when(away == 1)
             def _():
@@ -385,58 +432,50 @@
                 chain_out[step, rows:] = held[spot, rows:].astype(BF16)
                 chain_copy(step, 1).start()
 
+        @pl.when(step == 0)
+        def _():
+            send_later(2)
+
+        @pl.when(step == 1)
+        def _():
+            forward(0)
+            send_later(3)
+
         two = work_at(position - HOP2)
         away_two = split(jnp.maximum(two, 0))[3]
 
         @pl.when((two >= 0) & (away_two == 2))
         def _():
             for part in range(2):
-                pass_on(two, (position + 16 - HOP2) % 16, part)
+                pass_on(two, lax.bitwise_and(position + 16 - HOP2, 15), part)
 
         three = work_at(position - HOP3)
         away_three = split(jnp.maximum(three, 0))[3]
 
         @pl.when((three >= 0) & (away_three == 3))
         def _():
-            pass_on(three, (position + 16 - HOP3) % 16, 0)
+            pass_on(three, lax.bitwise_and(position + 16 - HOP3, 15), 0)
 
         @pl.when((three >= 0) & (away_three == 1))
         def _():
-            pass_on(three, (position + 16 - HOP3) % 16, 1)
+            pass_on(three, lax.bitwise_and(position + 16 - HOP3, 15), 1)
 
         four = work_at(position - HOP4)
-        _, w_four, group_four, away_four = split(jnp.maximum(four, 0))
+        _, tile_four, group_four, away_four = split(jnp.maximum(four, 0))
 
         @pl.when((four >= 0) & (away_four == 0))
         def _():
-            which = group_four * 2 + w_four
+            which = group_four * 4 + tile_four
             for part in range(2):
                 chain_copy(four, part).wait_recv()
             last_out[which] = (
-                held[(position + 16 - HOP4) % 16] + chain_in[four].astype(F32)
+                held[lax.bitwise_and(position + 16 - HOP4, 15)] + chain_in[four].astype(F32)
             ).astype(BF16)
-            here, copy = last_copy(w_four, group_four)
-
-            @pl.when(here)
-            def _():
-                last_in[zl, :, last_columns] = last_out[which]
-
-            @pl.when(jnp.logical_not(here))
-            def _():
-                copy.start()
+            send_last(tile_four, group_four)
 
         return carry
 
-    lax.fori_loop(0, len(ORDER) + HOP4, tick, 0)
-
-    for zs in range(2):
-        for cs in range(2):
-            @pl.when((near == 0) | (zs != zl) | (cs != core))
-            def _():
-                remote(
-                    last_out.at[0], last_in.at[zs, :, cs * half:(cs + 1) * half], last_send.at[0],
-                    last_recv.at[zs * 2 + cs], sibling,
-                ).wait_recv()
+    lax.fori_loop(0, PRODUCTS + PAUSES + HOP4, tick, 0)
 
     for copy in w_others:
         copy.wait_send()
@@ -447,35 +486,42 @@
             copy.wait_send()
         for dy in range(4):
             ks_copy(dz, dy).wait_send()
-    for part in range(2):
-        to_up(part).wait_send()
-        to_down(part).wait_send()
+    for q in range(CHUNKS):
+        if q >= 2:
+            to_up(q).wait_send()
+            to_down(q).wait_send()
         for slot in y_slot:
-            to_mate(slot, part).wait_send()
+            to_mate(slot, q).wait_send()
         for slot in range(8):
-            share_copy(slot, part).wait_send()
-    on_up().wait_send()
-    on_down().wait_send()
+            share_copy(slot, q).wait_send()
+        (on_up if q < CHUNKS // 2 else on_down)(q).wait_send()
 
     def drain(step, carry):
-        _, w, group, away = split(step)
+        _, tile, group, away = split(step)
 
         @pl.when(away != 0)
         def _():
             for part in range(2):
                 chain_copy(step, part).wait_send()
 
-        @pl.when(away == 0)
-        def _():
-            here, copy = last_copy(w, group)
-
-            @pl.when(jnp.logical_not(here))
+        @pl.when((away == 0) & jnp.logical_not(last_place(tile, group)[0]))
+        def _():
+            last_copy(tile, group, 0).wait_send()
+
+        return carry
+
+    lax.fori_loop(0, PRODUCTS, drain, 0)
+
+    for zs in range(2):
+        for cs in range(2):
+            @pl.when((near == 0) | (zs != zl) | (cs != core))
             def _():
-                copy.wait_send()
-
-        return carry
-
-    lax.fori_loop(0, 16, drain, 0)
+                for part in range(2):
+                    column = cs * half + part * 256
+                    remote(
+                        last_out.at[0], (low_in, high_in)[zs].at[:, column:column + 256],
+                        last_send.at[0], last_recv.at[zs * 2 + cs, part], sibling,
+                    ).wait_recv()
 
 
 def per_device(
@@ -488,11 +534,11 @@
     freq = jnp.asarray(np.tile(inverse_freq, (8, 2)), F32)
     anywhere = pl.BlockSpec(memory_space=pl.ANY)
     dma = pltpu.SemaphoreType.DMA
-    pieces = pl.pallas_call(
+    low, high = pl.pallas_call(
         kernel,
-        out_shape=jax.ShapeDtypeStruct((2, tokens, width), BF16),
+        out_shape=[jax.ShapeDtypeStruct((tokens, width), BF16)] * 2,
         in_specs=[anywhere] * 3 + [pl.BlockSpec(memory_space=pltpu.VMEM)] + [anywhere] * 4,
-        out_specs=pl.BlockSpec(memory_space=pltpu.VMEM),
+        out_specs=[pl.BlockSpec(memory_space=pltpu.VMEM)] * 2,
         scratch_shapes=[
             pltpu.SMEM(vertical_blocks.shape[::-1], jnp.int32),
             pltpu.SMEM(slash_offsets.shape[::-1], jnp.int32),
@@ -504,14 +550,14 @@
             pltpu.VMEM((32, 2, BLK, HD), BF16),
             pltpu.VMEM((8, tokens, 2 * depth), BF16),
             pltpu.VMEM((2, 2 * depth, half), BF16),
-            pltpu.VMEM((16, tokens, half), F32),
-            pltpu.VMEM((16, tokens, half), BF16),
-            pltpu.VMEM((16, tokens, half), BF16),
-            pltpu.VMEM((4, tokens, half), BF16),
-            dma((6,)), dma, dma((3,)), dma((3,)),
+            pltpu.VMEM((16, tokens, 256), F32),
+            pltpu.VMEM((PRODUCTS, tokens, 256), BF16),
+            pltpu.VMEM((PRODUCTS, tokens, 256), BF16),
+            pltpu.VMEM((8, tokens, 256), BF16),
+            dma((6,)), dma, dma((5,)), dma((5,)),
             dma((4,)), dma((4,)), dma((4, 3)), dma((4, 4)), dma((4, 4)), dma((4, 4)),
-            dma((8, 2)), dma((8, 2)), dma((8, 2)), dma((3, 2)), dma((8, 2)),
-            dma((16, 2)), dma((16, 2)), dma((4,)), dma((4,)),
+            dma((8, CHUNKS)), dma((8, CHUNKS)), dma((8, CHUNKS)), dma((3, CHUNKS)), dma((8, CHUNKS)),
+            dma((PRODUCTS, 2)), dma((PRODUCTS, 2)), dma((8,)), dma((4, 2)),
         ],
         compiler_params=pltpu.CompilerParams(
             collective_id=0, has_side_effects=True, vmem_limit_bytes=56 * 1024 * 1024
@@ -519,8 +565,8 @@
     )(
         vertical_blocks.T, slash_offsets.T, positions, freq, queries, key_states, value_states,
         out_weight,
-    ).astype(F32)
-    return (pieces[0] + pieces[1]).astype(BF16)
+    )
+    return (low.astype(F32) + high.astype(F32)).astype(BF16)
 
 
 def solution(mesh):

time: 139 us -> 126 us (0.906)
  Pallas kernels: 136 us -> 123 us
    pallas_call x1, Pallas kernels: 136 us -> 123 us  [per_device(): pl.pallas_call(kernel, out_shape=[jax.ShapeDtypeStruct((tokens, width), B...]
where the time goes in v4:
time: 126 us; the launch traced here: 125 us
  Pallas kernels  123 us (98%)
  other arithmetic  2.19 us (2%)
    pallas_call x1, Pallas kernels, per_device(): pl.pallas_call(kernel, out_shape=[jax.ShapeDtypeStruct((tokens, width), B...  123 us

profile of v4, /device:TPU:20, one launch (start us, length us, event | category | flops | bytes accessed | tf_op | source)
XLA Modules:
  0.0 125.5 jit_solution(12550432516005048486)
XLA Ops:
  0.0 123.2 %shard_map.82 = (bf16[256,1024]{1,0:T(8,128)(2,1)}, bf16[256,1024]{1,0:T(8,128)(2,1)}) custom-call(s32[4,8]{1,0:T(4,128)} %bitcast.2, s32[4,8]{1,0:T(4,128)} %bitcast.3, s32[256]{0:T(256)} %pos_in.1, f32[8,128]{1,0:T(8,128)} %constant.2.clone.freq_ref, bf16[256,1024]{1,0:T(8,128)(2,1)} %q_in.1, bf16[256,1024]{1,0:T(8,128)(2,1)} %k_ref.1, ...), custom_call_target="tpu_custom_call" | custom-call | tf_op jit(solution)/shard_map/pallas_call | solution.py:537
  123.3 2.2 %add_convert_fusion = bf16[256,1024]{1,0:T(8,128)(2,1)} fusion(bf16[256,1024]{1,0:T(8,128)(2,1)} %get-tuple-element.8, bf16[256,1024]{1,0:T(8,128)(2,1)} %get-tuple-element.7), kind=kLoop, calls=%fused_computation | loop fusion | flops 1048576 | bytes 1572864 | tf_op jit(solution)/shard_map/convert_element_type | solution.py:569

commit v5 on v4

--- a/solution.py
+++ b/solution.py
@@ -16,7 +16,8 @@
 
 HOP2, HOP3, HOP4 = 4, 9, 14
 PRODUCTS = 32
-PAUSES = 6
+FLUSH = 2
+PAUSES = 6 + FLUSH
 CHUNKS = 4
 
 
@@ -142,6 +143,9 @@
     kv[mine, 1] = v_own[...].astype(F32).T.astype(BF16)
     pl.semaphore_wait(barrier, 12 - near)
 
+    def all_of(ref, send, recv):
+        return remote(ref, ref, send, recv, sibling)
+
     def kz_copy(dz_there, index, where):
         return remote(kv.at[mine], kv.at[mine], kz_send.at[index], kz_recv.at[dz_there], where)
 
@@ -151,11 +155,11 @@
 
     def ky_copy(dz, dy, index, there, where):
         here = kv.at[block(dz, dy)]
-        return remote(here, here, ky_send.at[dz, index], ky_recv.at[dz, there], where)
+        return remote(here, here, ky_send, ky_recv.at[dz, there], where)
 
     def ks_copy(dz, dy):
         here = kv.at[block(dz, dy)]
-        return remote(here, here, ks_send.at[dz, dy], ks_recv.at[dz, dy], sibling)
+        return remote(here, here, ks_send, ks_recv, sibling)
 
     def kv_row(dz):
         return (ky_copy(dz, 0, 0, 3, y_up), ky_copy(dz, 0, 1, 1, y_down), ks_copy(dz, 0))
@@ -210,9 +214,7 @@
     for dz in range(4):
         ky_copy(dz, 2, 0, 2, sibling).wait_recv()
         ks_copy(dz, 2).start()
-    for dz in range(4):
-        for dy in range(4):
-            ks_copy(dz, dy).wait_recv()
+    all_of(kv.at[pl.ds(0, 16)], ks_send, ks_recv).wait_recv()
 
     def act_at(slot, part):
         return acts.at[slot, pl.ds(part * chunk, chunk), depth_here]
@@ -224,7 +226,7 @@
 
     def share_copy(slot, part):
         here = act_at(slot, part)
-        return remote(here, here, as_send.at[slot, part], as_recv.at[slot, part], sibling)
+        return remote(here, here, as_send, as_recv.at[slot, part], sibling)
 
     def act_wait(slot, part):
         act_copy(slot, slot, part, z_send.at[0, 0], sibling).wait_recv()
@@ -235,7 +237,7 @@
     on_up = lambda part: act_copy(3, 6, part, z_send.at[2, part], z_up)
     on_down = lambda part: act_copy(2, 6, part, z_send.at[2, part], z_down)
     y_slot = {0: 1, 2: 4, 3: 5, 6: 7}
-    to_mate = lambda slot, part: act_copy(slot, y_slot[slot], part, y_send.at[slot, part], y_mate)
+    to_mate = lambda slot, part: act_copy(slot, y_slot[slot], part, y_send, y_mate)
 
     ctx = zh * 4 + y
 
@@ -273,7 +275,7 @@
             acts[0, part * BLK:(part + 1) * BLK, column] = (mixed * (1.0 / total)).T.astype(BF16)
             return carry
 
-        lax.fori_loop(0, heads, one_head, 0, unroll=4)
+        lax.fori_loop(0, heads, one_head, 0, unroll=8)
 
     for part in range(2):
         attend(part)
@@ -318,7 +320,7 @@
     def chain_copy(step, part):
         here = pl.ds(part * rows, rows)
         return remote(
-            chain_out.at[step, here], chain_in.at[step, here], chain_send.at[step, part],
+            chain_out.at[step, here], chain_in.at[step, here], chain_send,
             chain_recv.at[step, part], x_down if part else x_up,
         )
 
@@ -332,7 +334,7 @@
     def last_copy(tile, group, zs):
         _, where, which, columns = last_place(tile, group)
         return remote(
-            last_out.at[which], (low_in, high_in)[zs].at[:, columns], last_send.at[which],
+            last_out.at[which], (low_in, high_in)[zs].at[:, columns], last_send,
             last_recv.at[zs * 2 + core, tile % 2], where,
         )
 
@@ -356,7 +358,10 @@
     def work_at(position):
         step = jnp.where(position < 2, position, -1)
         step = jnp.where((position >= 5) & (position < 7), position - 3, step)
-        step = jnp.where((position >= 10) & (position < PRODUCTS + PAUSES), position - PAUSES, step)
+        step = jnp.where((position >= 10) & (position < 18), position - 6, step)
+        step = jnp.where(
+            (position >= 18 + FLUSH) & (position < PRODUCTS + PAUSES), position - PAUSES, step
+        )
         return step
 
     def tick(position, carry):
@@ -380,7 +385,7 @@
             on_up(1).start()
             on_down(3).start()
 
-        @pl.when(step == 10)
+        @pl.when(position == 18 + FLUSH // 2)
         def _():
             forward_far(0)
             forward_far(2)
@@ -390,10 +395,21 @@
             forward_far(1)
             forward_far(3)
 
-        @pl.when((step == 2) | (step == 12) | (step == 15) | (step == 28))
+        @pl.when(step == 2)
         def _():
             for q in range(CHUNKS):
-                act_wait(slot, q)
+                act_wait(1, q)
+
+        @pl.when(step == 12)
+        def _():
+            for q in range(CHUNKS):
+                act_wait(4, q)
+                act_wait(5, q)
+
+        @pl.when(step == 27)
+        def _():
+            for q in range(CHUNKS):
+                act_wait(7, q)
 
         @pl.when((step >= 0) & (tile == 0))
         def _():
@@ -481,36 +497,24 @@
         copy.wait_send()
     for copy in kz_sends:
         copy.wait_send()
-    for dz in range(4):
-        for copy in kv_row(dz)[:2] + (kv_far(dz),):
-            copy.wait_send()
-        for dy in range(4):
-            ks_copy(dz, dy).wait_send()
+    all_of(kv.at[pl.ds(0, 12)], ky_send, ks_recv).wait_send()
+    all_of(kv.at[pl.ds(0, 16)], ks_send, ks_recv).wait_send()
     for q in range(CHUNKS):
         if q >= 2:
             to_up(q).wait_send()
             to_down(q).wait_send()
-        for slot in y_slot:
-            to_mate(slot, q).wait_send()
-        for slot in range(8):
-            share_copy(slot, q).wait_send()
         (on_up if q < CHUNKS // 2 else on_down)(q).wait_send()
-
-    def drain(step, carry):
-        _, tile, group, away = split(step)
-
-        @pl.when(away != 0)
-        def _():
-            for part in range(2):
-                chain_copy(step, part).wait_send()
-
-        @pl.when((away == 0) & jnp.logical_not(last_place(tile, group)[0]))
-        def _():
-            last_copy(tile, group, 0).wait_send()
-
-        return carry
-
-    lax.fori_loop(0, PRODUCTS, drain, 0)
+    all_of(acts.at[pl.ds(0, 4), :, depth_here], y_send, ks_recv).wait_send()
+    all_of(acts.at[:, :, depth_here], as_send, ks_recv).wait_send()
+    all_of(chain_out.at[pl.ds(0, PRODUCTS // 4 * 3)], chain_send, ks_recv).wait_send()
+
+    @pl.when(near == 1)
+    def _():
+        all_of(last_out.at[pl.ds(0, 6)], last_send, ks_recv).wait_send()
+
+    @pl.when(near == 0)
+    def _():
+        all_of(last_out, last_send, ks_recv).wait_send()
 
     for zs in range(2):
         for cs in range(2):
@@ -520,7 +524,7 @@
                     column = cs * half + part * 256
                     remote(
                         last_out.at[0], (low_in, high_in)[zs].at[:, column:column + 256],
-                        last_send.at[0], last_recv.at[zs * 2 + cs, part], sibling,
+                        last_send, last_recv.at[zs * 2 + cs, part], sibling,
                     ).wait_recv()
 
 
@@ -555,9 +559,9 @@
             pltpu.VMEM((PRODUCTS, tokens, 256), BF16),
             pltpu.VMEM((8, tokens, 256), BF16),
             dma((6,)), dma, dma((5,)), dma((5,)),
-            dma((4,)), dma((4,)), dma((4, 3)), dma((4, 4)), dma((4, 4)), dma((4, 4)),
-            dma((8, CHUNKS)), dma((8, CHUNKS)), dma((8, CHUNKS)), dma((3, CHUNKS)), dma((8, CHUNKS)),
-            dma((PRODUCTS, 2)), dma((PRODUCTS, 2)), dma((8,)), dma((4, 2)),
+            dma((4,)), dma((4,)), dma, dma((4, 4)), dma, dma,
+            dma((8, CHUNKS)), dma, dma((8, CHUNKS)), dma((3, CHUNKS)), dma,
+            dma, dma((PRODUCTS, 2)), dma, dma((4, 2)),
         ],
         compiler_params=pltpu.CompilerParams(
             collective_id=0, has_side_effects=True, vmem_limit_bytes=56 * 1024 * 1024

time: 126 us -> 121 us (0.960)
  Pallas kernels: 123 us -> 119 us
    pallas_call x1, Pallas kernels: 123 us -> 119 us  [per_device(): pl.pallas_call(kernel, out_shape=[jax.ShapeDtypeStruct((tokens, width), B...]
where the time goes in v5:
time: 121 us
  Pallas kernels  119 us (98%)
  other arithmetic  2.19 us (2%)
    pallas_call x1, Pallas kernels, per_device(): pl.pallas_call(kernel, out_shape=[jax.ShapeDtypeStruct((tokens, width), B...  119 us

profile of v5, /device:TPU:20, one launch (start us, length us, event | category | flops | bytes accessed | tf_op | source)
XLA Modules:
  0.0 121.2 jit_solution(7204319680241131760)
XLA Ops:
  0.0 119.0 %shard_map.82 = (bf16[256,1024]{1,0:T(8,128)(2,1)}, bf16[256,1024]{1,0:T(8,128)(2,1)}) custom-call(s32[4,8]{1,0:T(4,128)} %bitcast.2, s32[4,8]{1,0:T(4,128)} %bitcast.3, s32[256]{0:T(256)} %pos_in.1, f32[8,128]{1,0:T(8,128)} %constant.2.clone.freq_ref, bf16[256,1024]{1,0:T(8,128)(2,1)} %q_in.1, bf16[256,1024]{1,0:T(8,128)(2,1)} %k_ref.1, ...), custom_call_target="tpu_custom_call" | custom-call | tf_op jit(solution)/shard_map/pallas_call | solution.py:541
  119.0 2.2 %add_convert_fusion = bf16[256,1024]{1,0:T(8,128)(2,1)} fusion(bf16[256,1024]{1,0:T(8,128)(2,1)} %get-tuple-element.8, bf16[256,1024]{1,0:T(8,128)(2,1)} %get-tuple-element.7), kind=kLoop, calls=%fused_computation | loop fusion | flops 1048576 | bytes 1572864 | tf_op jit(solution)/shard_map/convert_element_type | solution.py:573

commit v6 on v5

--- a/solution.py
+++ b/solution.py
@@ -369,94 +369,6 @@
         slot, tile, group, away = split(jnp.maximum(step, 0))
         spot = lax.bitwise_and(position, 15)
 
-        @pl.when(step == 2)
-        def _():
-            forward(1)
-
-        @pl.when(step == 4)
-        def _():
-            forward(2)
-            on_up(0).start()
-            on_down(2).start()
-
-        @pl.when(step == 6)
-        def _():
-            forward(3)
-            on_up(1).start()
-            on_down(3).start()
-
-        @pl.when(position == 18 + FLUSH // 2)
-        def _():
-            forward_far(0)
-            forward_far(2)
-
-        @pl.when(step == 12)
-        def _():
-            forward_far(1)
-            forward_far(3)
-
-        @pl.when(step == 2)
-        def _():
-            for q in range(CHUNKS):
-                act_wait(1, q)
-
-        @pl.when(step == 12)
-        def _():
-            for q in range(CHUNKS):
-                act_wait(4, q)
-                act_wait(5, q)
-
-        @pl.when(step == 27)
-        def _():
-            for q in range(CHUNKS):
-                act_wait(7, q)
-
-        @pl.when((step >= 0) & (tile == 0))
-        def _():
-            for q in range(CHUNKS):
-                share_copy(slot, q).wait_recv()
-
-        @pl.when(step == 0)
-        def _():
-            w_own.wait()
-            w_others[0].wait_recv()
-
-        @pl.when(step == 4)
-        def _():
-            w_others[1].wait_recv()
-            w_others[2].wait_recv()
-
-        @pl.when(step == 21)
-        def _():
-            w_others[3].wait_recv()
-            w_others[4].wait_recv()
-
-        @pl.when(step >= 0)
-        def _():
-            column = pl.ds(pl.multiple_of(lax.bitwise_and(tile, 1) * 256, 256), 256)
-            held[spot] = jnp.dot(
-                acts[slot], weights[lax.shift_right_arithmetic(tile, 1), :, column], preferred_element_type=F32
-            )
-
-            @pl.when(away == 1)
-            def _():
-                chain_out[step, 0:rows] = held[spot, 0:rows].astype(BF16)
-                chain_copy(step, 0).start()
-
-            @pl.when(away == 3)
-            def _():
-                chain_out[step, rows:] = held[spot, rows:].astype(BF16)
-                chain_copy(step, 1).start()
-
-        @pl.when(step == 0)
-        def _():
-            send_later(2)
-
-        @pl.when(step == 1)
-        def _():
-            forward(0)
-            send_later(3)
-
         two = work_at(position - HOP2)
         away_two = split(jnp.maximum(two, 0))[3]
 
@@ -488,6 +400,94 @@
                 held[lax.bitwise_and(position + 16 - HOP4, 15)] + chain_in[four].astype(F32)
             ).astype(BF16)
             send_last(tile_four, group_four)
+
+        @pl.when(step == 2)
+        def _():
+            forward(1)
+
+        @pl.when(step == 4)
+        def _():
+            forward(2)
+            on_up(0).start()
+            on_down(2).start()
+
+        @pl.when(step == 6)
+        def _():
+            forward(3)
+            on_up(1).start()
+            on_down(3).start()
+
+        @pl.when(position == 18 + FLUSH // 2)
+        def _():
+            forward_far(0)
+            forward_far(2)
+
+        @pl.when(step == 12)
+        def _():
+            forward_far(1)
+            forward_far(3)
+
+        @pl.when(step == 2)
+        def _():
+            for q in range(CHUNKS):
+                act_wait(1, q)
+
+        @pl.when(step == 12)
+        def _():
+            for q in range(CHUNKS):
+                act_wait(4, q)
+                act_wait(5, q)
+
+        @pl.when(step == 27)
+        def _():
+            for q in range(CHUNKS):
+                act_wait(7, q)
+
+        @pl.when((step >= 0) & (tile == 0))
+        def _():
+            for q in range(CHUNKS):
+                share_copy(slot, q).wait_recv()
+
+        @pl.when(step == 0)
+        def _():
+            w_own.wait()
+            w_others[0].wait_recv()
+
+        @pl.when(step == 4)
+        def _():
+            w_others[1].wait_recv()
+            w_others[2].wait_recv()
+
+        @pl.when(step == 21)
+        def _():
+            w_others[3].wait_recv()
+            w_others[4].wait_recv()
+
+        @pl.when(step >= 0)
+        def _():
+            column = pl.ds(pl.multiple_of(lax.bitwise_and(tile, 1) * 256, 256), 256)
+            held[spot] = jnp.dot(
+                acts[slot], weights[lax.shift_right_arithmetic(tile, 1), :, column], preferred_element_type=F32
+            )
+
+            @pl.when(away == 1)
+            def _():
+                chain_out[step, 0:rows] = held[spot, 0:rows].astype(BF16)
+                chain_copy(step, 0).start()
+
+            @pl.when(away == 3)
+            def _():
+                chain_out[step, rows:] = held[spot, rows:].astype(BF16)
+                chain_copy(step, 1).start()
+
+        @pl.when(step == 0)
+        def _():
+            send_later(2)
+
+        @pl.when(step == 1)
+        def _():
+            forward(0)
+            send_later(3)
 
         return carry
 

time: 121 us -> 125 us (1.033)
  Pallas kernels: 119 us -> 122 us
    pallas_call x1, Pallas kernels: 119 us -> 122 us  [per_device(): pl.pallas_call(kernel, out_shape=[jax.ShapeDtypeStruct((tokens, width), B...]
where the time goes in v6:
time: 125 us
  Pallas kernels  122 us (98%)
  other arithmetic  2.19 us (2%)
    pallas_call x1, Pallas kernels, per_device(): pl.pallas_call(kernel, out_shape=[jax.ShapeDtypeStruct((tokens, width), B...  122 us

profile of v6, /device:TPU:20, one launch (start us, length us, event | category | flops | bytes accessed | tf_op | source)
XLA Modules:
  0.0 124.6 jit_solution(14960647778559598648)
XLA Ops:
  0.0 122.4 %shard_map.82 = (bf16[256,1024]{1,0:T(8,128)(2,1)}, bf16[256,1024]{1,0:T(8,128)(2,1)}) custom-call(s32[4,8]{1,0:T(4,128)} %bitcast.2, s32[4,8]{1,0:T(4,128)} %bitcast.3, s32[256]{0:T(256)} %pos_in.1, f32[8,128]{1,0:T(8,128)} %constant.2.clone.freq_ref, bf16[256,1024]{1,0:T(8,128)(2,1)} %q_in.1, bf16[256,1024]{1,0:T(8,128)(2,1)} %k_ref.1, ...), custom_call_target="tpu_custom_call" | custom-call | tf_op jit(solution)/shard_map/pallas_call | solution.py:541
  122.4 2.2 %add_convert_fusion = bf16[256,1024]{1,0:T(8,128)(2,1)} fusion(bf16[256,1024]{1,0:T(8,128)(2,1)} %get-tuple-element.8, bf16[256,1024]{1,0:T(8,128)(2,1)} %get-tuple-element.7), kind=kLoop, calls=%fused_computation | loop fusion | flops 1048576 | bytes 1572864 | tf_op jit(solution)/shard_map/convert_element_type | solution.py:573
